TPU v7x, 256 devices: a whole 4x4x8 slice. The times are simulated.
256 devices in a mesh: band: 32 (over z, x), wgrp: 8 (over y, core).
Axes of the slice: x: 4, y: 4, z: 8, core: 2. Of those that a mesh axis runs over, the one named last changes fastest.
Arguments:
- visibilities: bfloat16 [8, 2048, 512], P('wgrp', 'band'), may hold values from -6 to 6
- coordinates: bfloat16 [8, 2048, 512], P('wgrp', 'band'), may hold values from -16 to 16
- block_index: int32 [8, 8192], P('wgrp', 'band'), may hold values from 0 to 63
- counts: int32 [8, 1024], P('wgrp', 'band'), may hold values from 1 to 8, as said below
- col_offset: int32 [8, 8192], P('wgrp', 'band'), may hold values from 0 to 8160
Outputs:
- image_rows: float32 [8, 2, 1024, 8192], P('wgrp', None, 'band')
Inputs may be any that keep to these rules, and one draw needn't show every extreme that they name: Entry d of a device's row counts the live slots of its list for band d; every device's entry for band 32 // 2 is exactly 8. `block_index`: slots past a list's count read a block too; their subgrids are zero. `col_offset`: A subgrid lies inside its band's rows and the grid's columns.
All inputs are finite; a program needn't handle non-finite values.
Results may differ from a plain program's by a relative error of at most 0.0036.
Values may be sent and summed in bfloat16 or wider, within the bound.
A program may use at most 128 MiB of HBM per device.

v0:
```python
import math

import jax
import jax.numpy as jnp
from jax import lax
from jax.sharding import PartitionSpec as P

S = 32
G = 8192
K = 256
CAP = 8


TWO_PI = 2.0 * math.pi


def phase_tables(coord_rows):
    samples = coord_rows.shape[1] // 2
    pixel_pos = (jnp.arange(S, dtype=jnp.float32) - S / 2.0) * (TWO_PI / S)
    coords = coord_rows.astype(jnp.float32)
    angle_x = coords[:, None, :samples] * pixel_pos[None, :, None]
    angle_y = coords[:, None, samples:] * pixel_pos[None, :, None]
    return (angle_x, angle_y)


def weighted_rows(vis_rows, angle_x, angle_y):
    samples = vis_rows.shape[1] // 2
    vis_re = vis_rows[:, None, :samples].astype(jnp.float32)
    vis_im = vis_rows[:, None, samples:].astype(jnp.float32)
    cos_x = jnp.cos(angle_x)
    sin_x = jnp.sin(angle_x)
    weighted_re = (vis_re * cos_x - vis_im * sin_x).astype(jnp.bfloat16)
    weighted_im = (vis_re * sin_x + vis_im * cos_x).astype(jnp.bfloat16)
    cos_y = jnp.cos(angle_y).astype(jnp.bfloat16)
    sin_y = jnp.sin(angle_y).astype(jnp.bfloat16)
    return (weighted_re, weighted_im, cos_y, sin_y)


def product(left, right):
    return jnp.einsum("nyk,nxk->nyx", left, right, preferred_element_type=jnp.float32)


def block_subgrids(arrays):
    vis_rows, coord_rows = arrays
    angle_x, angle_y = phase_tables(coord_rows)
    weighted_re, weighted_im, cos_y, sin_y = weighted_rows(vis_rows, angle_x, angle_y)
    sub_re = product(cos_y, weighted_re) - product(sin_y, weighted_im)
    sub_im = product(cos_y, weighted_im) + product(sin_y, weighted_re)
    return jnp.stack([sub_re, sub_im], axis=1).reshape(vis_rows.shape[0], 2, S * S)


def blocked_subgrids(vis_rows, coord_rows):
    row_count = vis_rows.shape[0]
    block_rows = math.gcd(row_count, 64)
    turns = row_count // block_rows
    made = lax.map(
        block_subgrids,
        (vis_rows.reshape(turns, block_rows, -1), coord_rows.reshape(turns, block_rows, -1)),
    )
    return made.reshape(row_count, 2, S * S)


def row_transform(real_part, imag_part):
    row_count, length = real_part.shape
    inner_len = 128
    outer_len = length // inner_len
    highest = lax.Precision.HIGHEST
    first = jnp.arange(outer_len, dtype=jnp.int32)
    second = jnp.arange(inner_len, dtype=jnp.int32)
    angle_outer = (
        TWO_PI / outer_len * (first[:, None] * first[None, :] % outer_len).astype(jnp.float32)
    )
    angle_twist = TWO_PI / length * (first[:, None] * second[None, :] % length).astype(jnp.float32)
    angle_inner = (
        TWO_PI / inner_len * (second[:, None] * second[None, :] % inner_len).astype(jnp.float32)
    )
    cos_outer, sin_outer = (jnp.cos(angle_outer), jnp.sin(angle_outer))
    cos_twist, sin_twist = (jnp.cos(angle_twist), jnp.sin(angle_twist))
    cos_inner, sin_inner = (jnp.cos(angle_inner), jnp.sin(angle_inner))
    rows_re = real_part.reshape(row_count, outer_len, inner_len)
    rows_im = imag_part.reshape(row_count, outer_len, inner_len)
    section_re = jnp.einsum("kn,rnm->rkm", cos_outer, rows_re, precision=highest) + jnp.einsum(
        "kn,rnm->rkm", sin_outer, rows_im, precision=highest
    )
    section_im = jnp.einsum("kn,rnm->rkm", cos_outer, rows_im, precision=highest) - jnp.einsum(
        "kn,rnm->rkm", sin_outer, rows_re, precision=highest
    )
    twisted_re = section_re * cos_twist + section_im * sin_twist
    twisted_im = section_im * cos_twist - section_re * sin_twist
    out_re = jnp.einsum("rkn,nj->rjk", twisted_re, cos_inner, precision=highest) + jnp.einsum(
        "rkn,nj->rjk", twisted_im, sin_inner, precision=highest
    )
    out_im = jnp.einsum("rkn,nj->rjk", twisted_im, cos_inner, precision=highest) - jnp.einsum(
        "rkn,nj->rjk", twisted_re, sin_inner, precision=highest
    )
    return (out_re.reshape(row_count, length), out_im.reshape(row_count, length))


def shards(visibilities, coordinates, block_index, counts, col_offset):
    band_count = lax.axis_size("band")
    blocks = block_index[0]
    offsets = col_offset[0]
    slot_total = blocks.shape[0]
    slot_live = (jnp.arange(CAP, dtype=jnp.int32)[None, :] < counts[0][:, None]).reshape(-1)
    chosen_vis = jnp.take(visibilities[0], blocks, axis=0)
    chosen_coord = jnp.take(coordinates[0], blocks, axis=0)
    arrived_offsets = lax.all_to_all(offsets, "band", split_axis=0, concat_axis=0, tiled=True)
    computed = (
        blocked_subgrids(chosen_vis, chosen_coord) * slot_live.astype(jnp.float32)[:, None, None]
    )
    arrived = lax.all_to_all(computed, "band", split_axis=0, concat_axis=0, tiled=True)
    pixel_index = jnp.arange(S, dtype=jnp.int32)
    columns = (arrived_offsets[:, None] + pixel_index[None, :]).reshape(-1)
    values = jnp.transpose(arrived.reshape(slot_total, 2, S, S), (0, 3, 1, 2)).reshape(
        slot_total * S, 2 * S
    )
    placed = jnp.zeros((G, 2 * S), jnp.float32).at[columns].add(values)
    slab = jnp.transpose(placed, (1, 0)).reshape(2, S, G)[None]
    group_count = lax.axis_size("wgrp")
    spread = lax.all_to_all(
        lax.all_to_all(slab, "band", split_axis=3, concat_axis=2, tiled=True),
        "wgrp",
        split_axis=3,
        concat_axis=0,
        tiled=True,
    )
    spread = spread[::-1, :, ::-1, :]
    returned = lax.all_to_all(
        lax.all_to_all(spread, "band", split_axis=2, concat_axis=3, tiled=True),
        "wgrp",
        split_axis=0,
        concat_axis=3,
        tiled=True,
    )
    piece_width = G // (band_count * group_count)
    returned = returned.reshape(1, 2, S, group_count, band_count, piece_width)
    mirrored = jnp.swapaxes(returned, 3, 4).reshape(1, 2, S, G)[:, :, :, ::-1]
    spec_re, spec_im = row_transform(
        (slab[:, 0] + mirrored[:, 0]).reshape(-1, G), (slab[:, 1] - mirrored[:, 1]).reshape(-1, G)
    )
    norm_scale = 1.0 / math.sqrt(G * K)
    return (jnp.stack([spec_re, spec_im], axis=0) * norm_scale)[None]


def solution(mesh):
    placed = (
        P("wgrp", "band", None),
        P("wgrp", "band", None),
        P("wgrp", "band"),
        P("wgrp", "band"),
        P("wgrp", "band"),
    )
    return jax.shard_map(
        shards, mesh=mesh, in_specs=placed, out_specs=P("wgrp", None, "band", None), check_vma=False
    )
```

profile of v0, /device:TPU:1, one launch (start us, length us, event | category | flops | bytes accessed | tf_op | source)
XLA Modules:
  0.0 807.5 jit_solution(635368354494027602)
XLA Ops:
  2.6 11.9 %all-to-all-start = ((s32[32,8,1]{1,2,0:T(1,128)}), s32[32,8,1]{1,2,0:T(1,128)S(1)}, u32[]{:S(2)}, u32[]{:S(2)}) async-start(s32[32,8,1]{1,2,0:T(1,128)} %bitcast.6), calls=%async_computation | async-start | bytes 32768 | tf_op jit(solution)/shard_map/all_to_all | solution.py:107
  18.3 255.5 %while.12 = (s32[]{:T(128)}, f32[4,64,2,1024]{3,1,0,2:T(8,128)}, bf16[4,64,512]{2,1,0:T(8,128)(2,1)S(1)}, bf16[4,64,512]{2,1,0:T(8,128)(2,1)S(1)}, s32[]{:T(128)}) while((s32[]{:T(128)}, f32[4,64,2,1024]{3,1,0,2:T(8,128)}, bf16[4,64,512]{2,1,0:T(8,128)(2,1)S(1)}, bf16[4,64,512]{2,1,0:T(8,128)(2,1)S(1)}, s32[]{:T(128)}) %tuple.44), condition=%wide.region_1.3_spmd, body=%wide.region_0.0_spmd.sunk | while | flops 149225536 | bytes 7603393 | solution.py:56
  18.7 15.0 %fusion.140 = f32[64,32,32]{2,1,0:T(8,128)S(1)} fusion(f32[32]{0:T(128)S(1)} %add_multiply_fusion.2, f32[64,256]{1,0:T(8,128)S(1)} %get-tuple-element.114, f32[64,256]{1,0:T(8,128)S(1)} %get-tuple-element.116, f32[64,256]{1,0:T(8,128)S(1)} %get-tuple-element.117, f32[64,256]{1,0:T(8,128)S(1)} %get-tuple-element.118), kind=kOutput, calls=%fused_computation.20.clone.1 | convolution fusion | flops 37224448 | bytes 524416 | tf_op jit(solution)/shard_map/while/body/eval_jaxpr/nyk,nxk->nyx/dot_general | solution.py:40
  33.6 14.7 %convolution_subtract_fusion.4 = f32[64,32,32]{2,1,0:T(8,128)S(1)} fusion(f32[64,32,32]{2,1,0:T(8,128)S(1)} %fusion.140, f32[32]{0:T(128)S(1)} %add_multiply_fusion.2, f32[64,256]{1,0:T(8,128)S(1)} %get-tuple-element.114, f32[64,256]{1,0:T(8,128)S(1)} %get-tuple-element.116, f32[64,256]{1,0:T(8,128)S(1)} %get-tuple-element.117, ...), kind=kOutput, calls=%fused_computation.18.clone.1 | convolution fusion | flops 37289984 | bytes 786560 | tf_op jit(solution)/shard_map/while/body/eval_jaxpr/nyk,nxk->nyx/dot_general | solution.py:40
  48.9 14.8 %fusion.139 = f32[64,32,32]{2,1,0:T(8,128)S(1)} fusion(f32[32]{0:T(128)S(1)} %add_multiply_fusion.2, f32[64,256]{1,0:T(8,128)S(1)} %get-tuple-element.114, f32[64,256]{1,0:T(8,128)S(1)} %get-tuple-element.116, f32[64,256]{1,0:T(8,128)S(1)} %get-tuple-element.117, f32[64,256]{1,0:T(8,128)S(1)} %get-tuple-element.118), kind=kOutput, calls=%fused_computation.19.clone.1 | convolution fusion | flops 37224448 | bytes 524416 | tf_op jit(solution)/shard_map/while/body/eval_jaxpr/nyk,nxk->nyx/dot_general | solution.py:40
  63.8 14.7 %convolution_add_fusion.4 = f32[64,32,32]{2,1,0:T(8,128)S(1)} fusion(f32[64,32,32]{2,1,0:T(8,128)S(1)} %fusion.139, f32[32]{0:T(128)S(1)} %add_multiply_fusion.2, f32[64,256]{1,0:T(8,128)S(1)} %get-tuple-element.114, f32[64,256]{1,0:T(8,128)S(1)} %get-tuple-element.116, f32[64,256]{1,0:T(8,128)S(1)} %get-tuple-element.117, ...), kind=kOutput, calls=%fused_computation.17.clone.1 | convolution fusion | flops 37289984 | bytes 786560 | tf_op jit(solution)/shard_map/while/body/eval_jaxpr/nyk,nxk->nyx/dot_general | solution.py:40
  80.8 14.6 %fusion.140 = f32[64,32,32]{2,1,0:T(8,128)S(1)} fusion(f32[32]{0:T(128)S(1)} %add_multiply_fusion.2, f32[64,256]{1,0:T(8,128)S(1)} %get-tuple-element.114, f32[64,256]{1,0:T(8,128)S(1)} %get-tuple-element.116, f32[64,256]{1,0:T(8,128)S(1)} %get-tuple-element.117, f32[64,256]{1,0:T(8,128)S(1)} %get-tuple-element.118), kind=kOutput, calls=%fused_computation.20.clone.1 | convolution fusion | flops 37224448 | bytes 524416 | tf_op jit(solution)/shard_map/while/body/eval_jaxpr/nyk,nxk->nyx/dot_general | solution.py:40
  95.4 14.8 %convolution_subtract_fusion.4 = f32[64,32,32]{2,1,0:T(8,128)S(1)} fusion(f32[64,32,32]{2,1,0:T(8,128)S(1)} %fusion.140, f32[32]{0:T(128)S(1)} %add_multiply_fusion.2, f32[64,256]{1,0:T(8,128)S(1)} %get-tuple-element.114, f32[64,256]{1,0:T(8,128)S(1)} %get-tuple-element.116, f32[64,256]{1,0:T(8,128)S(1)} %get-tuple-element.117, ...), kind=kOutput, calls=%fused_computation.18.clone.1 | convolution fusion | flops 37289984 | bytes 786560 | tf_op jit(solution)/shard_map/while/body/eval_jaxpr/nyk,nxk->nyx/dot_general | solution.py:40
  110.8 14.9 %fusion.139 = f32[64,32,32]{2,1,0:T(8,128)S(1)} fusion(f32[32]{0:T(128)S(1)} %add_multiply_fusion.2, f32[64,256]{1,0:T(8,128)S(1)} %get-tuple-element.114, f32[64,256]{1,0:T(8,128)S(1)} %get-tuple-element.116, f32[64,256]{1,0:T(8,128)S(1)} %get-tuple-element.117, f32[64,256]{1,0:T(8,128)S(1)} %get-tuple-element.118), kind=kOutput, calls=%fused_computation.19.clone.1 | convolution fusion | flops 37224448 | bytes 524416 | tf_op jit(solution)/shard_map/while/body/eval_jaxpr/nyk,nxk->nyx/dot_general | solution.py:40
  125.7 14.7 %convolution_add_fusion.4 = f32[64,32,32]{2,1,0:T(8,128)S(1)} fusion(f32[64,32,32]{2,1,0:T(8,128)S(1)} %fusion.139, f32[32]{0:T(128)S(1)} %add_multiply_fusion.2, f32[64,256]{1,0:T(8,128)S(1)} %get-tuple-element.114, f32[64,256]{1,0:T(8,128)S(1)} %get-tuple-element.116, f32[64,256]{1,0:T(8,128)S(1)} %get-tuple-element.117, ...), kind=kOutput, calls=%fused_computation.17.clone.1 | convolution fusion | flops 37289984 | bytes 786560 | tf_op jit(solution)/shard_map/while/body/eval_jaxpr/nyk,nxk->nyx/dot_general | solution.py:40
  142.7 14.6 %fusion.140 = f32[64,32,32]{2,1,0:T(8,128)S(1)} fusion(f32[32]{0:T(128)S(1)} %add_multiply_fusion.2, f32[64,256]{1,0:T(8,128)S(1)} %get-tuple-element.114, f32[64,256]{1,0:T(8,128)S(1)} %get-tuple-element.116, f32[64,256]{1,0:T(8,128)S(1)} %get-tuple-element.117, f32[64,256]{1,0:T(8,128)S(1)} %get-tuple-element.118), kind=kOutput, calls=%fused_computation.20.clone.1 | convolution fusion | flops 37224448 | bytes 524416 | tf_op jit(solution)/shard_map/while/body/eval_jaxpr/nyk,nxk->nyx/dot_general | solution.py:40
  157.3 14.8 %convolution_subtract_fusion.4 = f32[64,32,32]{2,1,0:T(8,128)S(1)} fusion(f32[64,32,32]{2,1,0:T(8,128)S(1)} %fusion.140, f32[32]{0:T(128)S(1)} %add_multiply_fusion.2, f32[64,256]{1,0:T(8,128)S(1)} %get-tuple-element.114, f32[64,256]{1,0:T(8,128)S(1)} %get-tuple-element.116, f32[64,256]{1,0:T(8,128)S(1)} %get-tuple-element.117, ...), kind=kOutput, calls=%fused_computation.18.clone.1 | convolution fusion | flops 37289984 | bytes 786560 | tf_op jit(solution)/shard_map/while/body/eval_jaxpr/nyk,nxk->nyx/dot_general | solution.py:40
  172.7 14.9 %fusion.139 = f32[64,32,32]{2,1,0:T(8,128)S(1)} fusion(f32[32]{0:T(128)S(1)} %add_multiply_fusion.2, f32[64,256]{1,0:T(8,128)S(1)} %get-tuple-element.114, f32[64,256]{1,0:T(8,128)S(1)} %get-tuple-element.116, f32[64,256]{1,0:T(8,128)S(1)} %get-tuple-element.117, f32[64,256]{1,0:T(8,128)S(1)} %get-tuple-element.118), kind=kOutput, calls=%fused_computation.19.clone.1 | convolution fusion | flops 37224448 | bytes 524416 | tf_op jit(solution)/shard_map/while/body/eval_jaxpr/nyk,nxk->nyx/dot_general | solution.py:40
  187.5 14.7 %convolution_add_fusion.4 = f32[64,32,32]{2,1,0:T(8,128)S(1)} fusion(f32[64,32,32]{2,1,0:T(8,128)S(1)} %fusion.139, f32[32]{0:T(128)S(1)} %add_multiply_fusion.2, f32[64,256]{1,0:T(8,128)S(1)} %get-tuple-element.114, f32[64,256]{1,0:T(8,128)S(1)} %get-tuple-element.116, f32[64,256]{1,0:T(8,128)S(1)} %get-tuple-element.117, ...), kind=kOutput, calls=%fused_computation.17.clone.1 | convolution fusion | flops 37289984 | bytes 786560 | tf_op jit(solution)/shard_map/while/body/eval_jaxpr/nyk,nxk->nyx/dot_general | solution.py:40
  204.6 14.6 %fusion.140 = f32[64,32,32]{2,1,0:T(8,128)S(1)} fusion(f32[32]{0:T(128)S(1)} %add_multiply_fusion.2, f32[64,256]{1,0:T(8,128)S(1)} %get-tuple-element.114, f32[64,256]{1,0:T(8,128)S(1)} %get-tuple-element.116, f32[64,256]{1,0:T(8,128)S(1)} %get-tuple-element.117, f32[64,256]{1,0:T(8,128)S(1)} %get-tuple-element.118), kind=kOutput, calls=%fused_computation.20.clone.1 | convolution fusion | flops 37224448 | bytes 524416 | tf_op jit(solution)/shard_map/while/body/eval_jaxpr/nyk,nxk->nyx/dot_general | solution.py:40
  219.2 14.8 %convolution_subtract_fusion.4 = f32[64,32,32]{2,1,0:T(8,128)S(1)} fusion(f32[64,32,32]{2,1,0:T(8,128)S(1)} %fusion.140, f32[32]{0:T(128)S(1)} %add_multiply_fusion.2, f32[64,256]{1,0:T(8,128)S(1)} %get-tuple-element.114, f32[64,256]{1,0:T(8,128)S(1)} %get-tuple-element.116, f32[64,256]{1,0:T(8,128)S(1)} %get-tuple-element.117, ...), kind=kOutput, calls=%fused_computation.18.clone.1 | convolution fusion | flops 37289984 | bytes 786560 | tf_op jit(solution)/shard_map/while/body/eval_jaxpr/nyk,nxk->nyx/dot_general | solution.py:40
  234.5 14.9 %fusion.139 = f32[64,32,32]{2,1,0:T(8,128)S(1)} fusion(f32[32]{0:T(128)S(1)} %add_multiply_fusion.2, f32[64,256]{1,0:T(8,128)S(1)} %get-tuple-element.114, f32[64,256]{1,0:T(8,128)S(1)} %get-tuple-element.116, f32[64,256]{1,0:T(8,128)S(1)} %get-tuple-element.117, f32[64,256]{1,0:T(8,128)S(1)} %get-tuple-element.118), kind=kOutput, calls=%fused_computation.19.clone.1 | convolution fusion | flops 37224448 | bytes 524416 | tf_op jit(solution)/shard_map/while/body/eval_jaxpr/nyk,nxk->nyx/dot_general | solution.py:40
  249.4 14.7 %convolution_add_fusion.4 = f32[64,32,32]{2,1,0:T(8,128)S(1)} fusion(f32[64,32,32]{2,1,0:T(8,128)S(1)} %fusion.139, f32[32]{0:T(128)S(1)} %add_multiply_fusion.2, f32[64,256]{1,0:T(8,128)S(1)} %get-tuple-element.114, f32[64,256]{1,0:T(8,128)S(1)} %get-tuple-element.116, f32[64,256]{1,0:T(8,128)S(1)} %get-tuple-element.117, ...), kind=kOutput, calls=%fused_computation.17.clone.1 | convolution fusion | flops 37289984 | bytes 786560 | tf_op jit(solution)/shard_map/while/body/eval_jaxpr/nyk,nxk->nyx/dot_general | solution.py:40
  278.7 9.3 %all-to-all-start.1 = ((f32[256,2,1024]{2,1,0:T(2,128)}), f32[256,2,1024]{2,1,0:T(2,128)}, u32[]{:S(2)}, u32[]{:S(2)}) async-start(f32[256,2,1024]{2,1,0:T(2,128)} %copy.37), calls=%async_computation.1 | async-start | bytes 4194304 | tf_op jit(solution)/shard_map/all_to_all | solution.py:111
  289.1 46.9 %all-to-all-done.1 = f32[256,2,1024]{2,1,0:T(2,128)} async-done(((f32[256,2,1024]{2,1,0:T(2,128)}), f32[256,2,1024]{2,1,0:T(2,128)}, u32[]{:S(2)}, u32[]{:S(2)}) %all-to-all-start.1) | async-done | bytes 2097184 | tf_op jit(solution)/shard_map/all_to_all | solution.py:111
  338.8 6.4 copy.53
  345.2 8.8 %reshape.230 = f32[8192,64]{1,0:T(8,128)} reshape(f32[256,32,2,32]{3,2,1,0:T(2,128)} %copy.53) | data formatting | bytes 4194304 | tf_op jit(solution)/shard_map/reshape | solution.py:114
  354.0 46.5 %scatter_custom_fusion = f32[8192,64]{1,0:T(8,128)} fusion(s32[8192]{0:T(1024)S(1)} %bitcast.121, f32[8192,64]{1,0:T(8,128)} %reshape.230, f32[]{:T(128)} %constant.88.clone.1), kind=kCustom, calls=%fused_computation.39 | custom fusion | flops 524288 | bytes 2097664 | tf_op jit(solution)/shard_map/scatter-add | solution.py:117
  403.3 7.9 copy.42
  411.2 10.8 %reshape.249 = f32[32,1,16384]{2,1,0:T(1,128)} reshape(f32[8192,1,2,32]{3,2,1,0:T(2,128)} %bitcast.105) | data formatting | bytes 4194304
  422.1 54.2 %all_to_all.83 = f32[32,1,16384]{2,1,0:T(1,128)} all-to-all(f32[32,1,16384]{2,1,0:T(1,128)} %reshape.249), channel_id=1, replica_groups=mesh['band'=32,'wgrp'=8] {'band'}, dimensions={0} | all-to-all | bytes 4194304 | tf_op jit(solution)/shard_map/all_to_all | solution.py:121
  476.8 8.7 %reduce.8 = f32[32,16384]{1,0:T(8,128)} reduce(f32[32,1,16384]{2,1,0:T(1,128)} %all_to_all.83, f32[]{:T(128)} %broadcast.179), dimensions={1}, to_apply=%all_to_all.62.reduce_sub_computation | reduce | bytes 4194308 | tf_op jit(solution)/shard_map/all_to_all | solution.py:121
  485.5 9.5 %reshape.250 = f32[8192,1,2,32]{3,2,1,0:T(2,128)} reshape(f32[32,16384]{1,0:T(8,128)} %reduce.8) | data formatting | bytes 4194304
  495.0 10.9 %copy.55 = f32[1,2,32,32,256]{4,2,3,1,0:T(8,128)} copy(f32[1,2,32,32,256]{2,1,4,3,0:T(2,128)} %bitcast.103) | data formatting | bytes 4194304 | tf_op jit(solution)/shard_map/all_to_all | solution.py:121
  505.9 4.2 copy.45
  510.0 34.9 %all_to_all.84 = f32[1,2,1024,256]{2,1,0,3:T(2,128)S(1)} all-to-all(f32[1,2,1024,256]{2,1,0,3:T(2,128)} %copy.45), channel_id=1, replica_groups=mesh['band'=32,'wgrp'=8] {'wgrp'}, dimensions={3} | all-to-all | bytes 4194304 | tf_op jit(solution)/shard_map/all_to_all | solution.py:120
  546.9 6.1 rev.4
  553.0 7.4 copy.47
  560.5 7.7 reshape.251
  568.2 54.3 %all_to_all.85 = f32[32,1,16384]{2,1,0:T(1,128)} all-to-all(f32[32,1,16384]{2,1,0:T(1,128)} %reshape.251), channel_id=1, replica_groups=mesh['band'=32,'wgrp'=8] {'band'}, dimensions={0} | all-to-all | bytes 4194304 | tf_op jit(solution)/shard_map/all_to_all | solution.py:129
  622.5 8.7 %reduce.9 = f32[32,16384]{1,0:T(8,128)} reduce(f32[32,1,16384]{2,1,0:T(1,128)} %all_to_all.85, f32[]{:T(128)} %broadcast.179), dimensions={1}, to_apply=%all_to_all.70.reduce_sub_computation | reduce | bytes 4194308 | tf_op jit(solution)/shard_map/all_to_all | solution.py:129
  631.2 6.4 reshape.252
  637.6 11.5 %copy.62 = f32[8,2,32,32,32]{4,2,3,1,0:T(8,128)} copy(f32[8,2,32,32,32]{4,0,1,3,2:T(8,128)} %bitcast.106) | data formatting | bytes 4194304 | tf_op jit(solution)/shard_map/all_to_all | solution.py:129
  649.0 7.8 all_to_all.73
  656.9 7.2 all-to-all-start.5
  664.3 26.2 %all-to-all-done.5 = f32[8,2,32,1024]{3,2,1,0:T(8,128)} async-done(((f32[8,2,32,1024]{3,2,1,0:T(8,128)}), f32[8,2,32,1024]{3,2,1,0:T(8,128)}, u32[]{:S(2)}, u32[]{:S(2)}) %all-to-all-start.5) | async-done | bytes 2097184 | tf_op jit(solution)/shard_map/all_to_all | solution.py:128
  690.5 4.1 copy.49
  694.6 6.5 reshape.192
  701.1 14.7 %copy.50 = f32[1,2,32,32,8,32]{5,4,3,2,1,0:T(8,128)} copy(f32[1,2,32,32,8,32]{5,3,4,2,1,0:T(8,128)} %bitcast.108) | data formatting | bytes 4194304 | tf_op jit(solution)/shard_map/transpose | solution.py:137
  715.8 7.4 reshape.193
  726.2 25.3 %slice.44 = f32[1,1,32,8192]{3,2,1,0:T(8,128)S(1)} reverse(f32[1,1,32,8192]{3,2,1,0:T(8,128)} %get-tuple-element.77), dimensions={3} | reverse | bytes 2097152 | tf_op jit(solution)/shard_map/slice | solution.py:139
  751.5 30.6 %slice.47 = f32[1,1,32,8192]{3,2,1,0:T(8,128)} reverse(f32[1,1,32,8192]{3,2,1,0:T(8,128)} %get-tuple-element.76), dimensions={3} | reverse | bytes 2097152 | tf_op jit(solution)/shard_map/slice | solution.py:139
  797.6 3.4 fusion.30
  (85 shorter events, 55.0 us)
Async XLA Ops:
  0.0 15.8 %copy-start = (bf16[1,64,512]{2,1,0:T(8,128)(2,1)S(1)}, bf16[1,64,512]{2,1,0:T(8,128)(2,1)}, u32[]{:S(2)}) copy-start(bf16[1,64,512]{2,1,0:T(8,128)(2,1)} %param.10) | copy-start | bytes 196612
  0.0 17.0 %copy-start.2 = (bf16[1,64,512]{2,1,0:T(8,128)(2,1)S(1)}, bf16[1,64,512]{2,1,0:T(8,128)(2,1)}, u32[]{:S(2)}) copy-start(bf16[1,64,512]{2,1,0:T(8,128)(2,1)} %param.9) | copy-start | bytes 196612
  2.6 276.1 %all-to-all-start = ((s32[32,8,1]{1,2,0:T(1,128)}), s32[32,8,1]{1,2,0:T(1,128)S(1)}, u32[]{:S(2)}, u32[]{:S(2)}) async-start(s32[32,8,1]{1,2,0:T(1,128)} %bitcast.6), calls=%async_computation | async-start | bytes 32768 | tf_op jit(solution)/shard_map/all_to_all | solution.py:107
  18.3 255.5 %copy-start.3 = (s32[1,32]{1,0:T(1,128)S(1)}, s32[1,32]{1,0:T(1,128)}, u32[]{:S(2)}) copy-start(s32[1,32]{1,0:T(1,128)} %param.12) | copy-start | bytes 388
  278.7 57.3 %all-to-all-start.1 = ((f32[256,2,1024]{2,1,0:T(2,128)}), f32[256,2,1024]{2,1,0:T(2,128)}, u32[]{:S(2)}, u32[]{:S(2)}) async-start(f32[256,2,1024]{2,1,0:T(2,128)} %copy.37), calls=%async_computation.1 | async-start | bytes 4194304 | tf_op jit(solution)/shard_map/all_to_all | solution.py:111
  656.9 33.6 %all-to-all-start.5 = ((f32[8,2,32,1024]{3,2,1,0:T(8,128)}), f32[8,2,32,1024]{3,2,1,0:T(8,128)}, u32[]{:S(2)}, u32[]{:S(2)}) async-start(f32[8,2,32,1024]{3,2,1,0:T(8,128)} %all_to_all.73), calls=%async_computation.5 | async-start | bytes 4194304 | tf_op jit(solution)/shard_map/all_to_all | solution.py:128
  802.8 4.4 copy-start.1
where the time goes:
time: 816 us; the launch traced here: 807 us
  matrix products  249 us (31%)
  local copies, waits for them, and re-layouts  230 us (28%)
  blocking collectives  143 us (18%)
  other arithmetic  74.1 us (9%)
  waiting for transfers between devices  73.1 us (9%)
  starting transfers between devices  28.4 us (3%)
  loops' own time  9.47 us (1%)
    dot_general x16, matrix products, product(): jnp.einsum('nyk,nxk->nyx', left, right, preferred_element_type=jnp.float32)  236 us
    all_to_all x1, blocking collectives, shards(): lax.all_to_all(spread, 'band', split_axis=2, concat_axis=3, tiled=True)  54.3 us
    all_to_all x1, blocking collectives, shards(): lax.all_to_all(slab, 'band', split_axis=3, concat_axis=2, tiled=True)  54.2 us
    all_to_all x1, waiting for transfers between devices, shards(): lax.all_to_all(computed, 'band', split_axis=0, concat_axis=0, tiled=True)  46.9 us
    scatter-add x1, other arithmetic, shards(): placed = jnp.zeros((G, 2 * S), jnp.float32).at[columns].add(values)  46.5 us
    unnamed x15, local copies, waits for them, and re-layouts  35.5 us
    all_to_all x1, blocking collectives, shards(): lax.all_to_all(lax.all_to_all(slab, 'band', split_axis=3, concat_axis=2,...  34.9 us
    slice x2, local copies, waits for them, and re-layouts, shards(): mirrored[:, 1]  33.6 us
  transfers between devices with their start and end apart: 3, of which 2 were waited for; matrix products, arithmetic and copies ran while one was open for 32% of the time, Pallas kernels for 0%

commit v1 on v0

v1 whole, which is shorter than its diff:
```python
import functools
import math

import jax
import jax.numpy as jnp
import numpy as np
from jax import lax
from jax.experimental import pallas as pl
from jax.experimental.pallas import tpu as pltpu
from jax.sharding import PartitionSpec as P

S = 32
G = 8192
K = 256
CAP = 8
NBLK = 64
LANES = 128
TILES = G // LANES
HALF = S // 2
MESH = pl.DeviceIdType.MESH
F32 = jnp.float32
BF16 = jnp.bfloat16


def fit(func, degree):
    nodes = 0.125 + 0.125 * np.cos(np.pi * (np.arange(400) + 0.5) / 400)
    series = np.polynomial.chebyshev.Chebyshev.fit(nodes, func(nodes), degree, domain=[0, 0.25])
    return [float(c) for c in series.convert(kind=np.polynomial.Polynomial).coef]


SIN_COEF = fit(lambda q: np.sin(2 * np.pi * np.sqrt(q)) / np.sqrt(q), 6)
COS_COEF = fit(lambda q: np.cos(2 * np.pi * np.sqrt(q)), 7)


def horner(coef, q):
    total = jnp.full_like(q, coef[-1])
    for c in coef[-2::-1]:
        total = total * q + c
    return total


def unit(cycles):
    frac = cycles - jnp.floor(cycles + 0.5)
    q = frac * frac
    return horner(COS_COEF, q), frac * horner(SIN_COEF, q)


def cmul(a, b):
    return a[0] * b[0] - a[1] * b[1], a[0] * b[1] + a[1] * b[0]


def subgrid_kernel(index_ref, counts_ref, vis_ref, coord_ref, out_ref, vf_ref, cf_ref, z_ref, sub_ref):
    vf_ref[...] = vis_ref[...].astype(F32)
    cf_ref[...] = coord_ref[...].astype(F32)
    for axis in range(2):
        pos = cf_ref[:, axis * K : (axis + 1) * K]
        for which, step in enumerate((1.0, 8.0, 16.0)):
            re, im = unit(pos * (step / S))
            z_ref[axis, which, 0] = re
            z_ref[axis, which, 1] = im
    eighth = lax.broadcasted_iota(jnp.int32, (8, K), 0).astype(F32) * (1.0 / S)
    sub_ref[:, NBLK] = jnp.zeros((2, S, LANES), BF16)

    def one_block(m):
        row = pl.ds(m, 1)

        def powers(axis, which):
            return z_ref[axis, which, 0, row, :], z_ref[axis, which, 1, row, :]

        base = unit(cf_ref[row, 0:K] * eighth)
        z8 = powers(0, 1)
        z16 = powers(0, 2)
        rr, ii, ri, ir = z8[0] * base[0], z8[1] * base[1], z8[0] * base[1], z8[1] * base[0]
        low = (z16[0] * base[0] + z16[1] * base[1], z16[0] * base[1] - z16[1] * base[0])
        parts = (low, (rr + ii, ri - ir), base, (rr - ii, ri + ir))
        vis = (vf_ref[row, 0:K], vf_ref[row, K : 2 * K])
        mirrored = cmul((vis[0], -vis[1]), powers(0, 0))
        weights = []
        for factor in (vis, mirrored):
            made = [cmul(factor, part) for part in parts]
            weights.append(
                jnp.concatenate(
                    [jnp.concatenate([c[0] for c in made], 0), jnp.concatenate([c[1] for c in made], 0)], 1
                ).astype(BF16)
            )
        base = unit(cf_ref[row, K : 2 * K] * eighth)
        z8 = powers(1, 1)
        z16 = powers(1, 2)
        pair = (
            cmul((z16[0], -z16[1]), base),
            cmul((z8[0], -z8[1]), base),
        )
        table = (jnp.concatenate([pair[0][0], pair[1][0]], 0), jnp.concatenate([pair[0][1], pair[1][1]], 0))
        rows = []
        for cos, sin in (table, cmul(powers(1, 0), table)):
            rows.append(jnp.concatenate([cos, -sin], 1))
            rows.append(jnp.concatenate([sin, cos], 1))
        left = jnp.concatenate(rows, 0).astype(BF16)
        right = jnp.concatenate(weights, 0)
        made = lax.dot_general(left, right, (((1,), (1,)), ((), ())), preferred_element_type=F32)
        for half in range(2):
            piece = made[half * S : (half + 1) * S, half * S : (half + 1) * S]
            sub_ref[half, m] = jnp.concatenate([piece] * 4, 1).astype(BF16)

    def some_blocks(i, carry):
        for j in range(2):
            one_block(i * 2 + j)
        return carry

    lax.fori_loop(0, NBLK // 2, some_blocks, 0)
    lane = lax.broadcasted_iota(jnp.int32, (S, LANES), 1) // S

    def expand(d, carry):
        live = counts_ref[0, d]
        for group in range(2):
            idx = []
            for j in range(4):
                slot = group * 4 + j
                idx.append(jnp.where(slot < live, index_ref[0, d * CAP + slot], NBLK))
            for half in range(2):
                value = sub_ref[half, idx[3]]
                for j in range(3):
                    value = jnp.where(lane == j, sub_ref[half, idx[j]], value)
                out_ref[half, d, group] = value
        return carry

    lax.fori_loop(0, S, expand, 0)


def make_subgrids(vis, coord, index, counts):
    vmem = pl.BlockSpec(memory_space=pltpu.VMEM)
    smem = pl.BlockSpec(memory_space=pltpu.SMEM)
    return pl.pallas_call(
        subgrid_kernel,
        out_shape=jax.ShapeDtypeStruct((2, S, 2, S, LANES), BF16),
        in_specs=[smem, smem, vmem, vmem],
        out_specs=vmem,
        scratch_shapes=[
            pltpu.VMEM((NBLK, 2 * K), F32),
            pltpu.VMEM((NBLK, 2 * K), F32),
            pltpu.VMEM((2, 3, 2, NBLK, K), F32),
            pltpu.VMEM((2, NBLK + 1, S, LANES), BF16),
        ],
        name="subgrids",
    )(index, counts, vis, coord)


def exchange_kernel(send_ref, offs_ref, recv_ref, roff_ref, send_sem, recv_sem, osend_sem, orecv_sem, own_sem):
    band = lax.axis_index("band")
    plane = lax.axis_index("wgrp")
    z = band // 4
    x = band % 4

    def peer(j):
        turn = j // 8
        dz = 4 + ((turn + 1) // 2) * (2 * (turn % 2) - 1)
        dx = 3 - (j // 2) % 4
        half = 1 - j % 2
        return half, ((z + dz) % 8) * 4 + (x + dx) % 4

    def device(half, d):
        return (d + half * (31 - 2 * d), plane + half * (7 - 2 * plane))

    barrier = pltpu.get_barrier_semaphore()

    def greet(j, carry):
        half, d = peer(j)
        pl.semaphore_signal(barrier, inc=1, device_id=device(half, d), device_id_type=MESH)
        return carry

    lax.fori_loop(0, 63, greet, 0)
    own = pltpu.make_async_copy(send_ref.at[0, band], recv_ref.at[0, band], own_sem.at[0])
    own.start()
    own_offs = pltpu.make_async_copy(offs_ref.at[0, band], roff_ref.at[0, band], own_sem.at[1])
    own_offs.start()
    pl.semaphore_wait(barrier, 63)

    def copies(j):
        half, d = peer(j)
        data = pltpu.make_async_remote_copy(
            src_ref=send_ref.at[half, d],
            dst_ref=recv_ref.at[half, band],
            send_sem=send_sem.at[half, d],
            recv_sem=recv_sem.at[half, band],
            device_id=device(half, d),
            device_id_type=MESH,
        )
        offs = pltpu.make_async_remote_copy(
            src_ref=offs_ref.at[half, d],
            dst_ref=roff_ref.at[half, band],
            send_sem=osend_sem.at[half, d],
            recv_sem=orecv_sem.at[half, band],
            device_id=device(half, d),
            device_id_type=MESH,
        )
        return data, offs

    def start(j, carry):
        data, offs = copies(j)
        data.start()
        offs.start()
        return carry

    lax.fori_loop(0, 63, start, 0)
    own.wait()
    own_offs.wait()

    def finish(j, carry):
        half, d = peer(j)
        data, offs = copies(j)
        data.wait_send()
        offs.wait_send()
        for dst, sem, src in ((recv_ref, recv_sem, send_ref), (roff_ref, orecv_sem, offs_ref)):
            pltpu.make_async_remote_copy(
                src_ref=src.at[half, d],
                dst_ref=dst.at[half, d],
                send_sem=send_sem.at[half, d],
                recv_sem=sem.at[half, d],
                device_id=device(half, d),
                device_id_type=MESH,
            ).wait_recv()
        return carry

    lax.fori_loop(0, 63, finish, 0)


def exchange(lists, offsets):
    anywhere = pl.BlockSpec(memory_space=pl.ANY)
    return pl.pallas_call(
        exchange_kernel,
        out_shape=(
            jax.ShapeDtypeStruct(lists.shape, lists.dtype),
            jax.ShapeDtypeStruct(offsets.shape, offsets.dtype),
        ),
        in_specs=[anywhere, anywhere],
        out_specs=(anywhere, anywhere),
        scratch_shapes=[pltpu.SemaphoreType.DMA((2, S))] * 4 + [pltpu.SemaphoreType.DMA((2,))],
        compiler_params=pltpu.CompilerParams(collective_id=0, has_side_effects=True),
        name="exchange",
    )(lists, offsets)


def place_kernel(offs_ref, lists_ref, out_ref, low_ref, *slabs):
    zero = jnp.zeros((S, LANES), F32)

    def clear(t, carry):
        for slab in slabs:
            slab[t] = zero
        return carry

    lax.fori_loop(0, TILES + 1, clear, 0)
    lane = lax.broadcasted_iota(jnp.int32, (S, LANES), 1)

    def place(i, carry):
        half = i // (2 * S)
        source = (i // 2) % S
        group = i % 2
        values = lists_ref[half, source, group].astype(F32)
        for j, slab in enumerate(slabs):
            start = offs_ref[half, source, 0, group * 4 + j]
            tile = start // LANES
            first = start % LANES
            turned = pltpu.roll(values, (first + LANES - S * j) % LANES, 1)
            slab[tile] += jnp.where((lane >= first) & (lane < first + S), turned, zero)
            slab[tile + 1] += jnp.where(lane < first + S - LANES, turned, zero)
        return carry

    lax.fori_loop(0, 4 * S, place, 0, unroll=2)

    def gather(t, carry):
        total = (slabs[0][t] + slabs[1][t]) + (slabs[2][t] + slabs[3][t])
        out_ref[t] = total
        low_ref[t] = total.astype(BF16)
        return carry

    lax.fori_loop(0, TILES, gather, 0)


def place(offsets, lists):
    vmem = pl.BlockSpec(memory_space=pltpu.VMEM)
    return pl.pallas_call(
        place_kernel,
        out_shape=(
            jax.ShapeDtypeStruct((TILES, S, LANES), F32),
            jax.ShapeDtypeStruct((TILES, S, LANES), BF16),
        ),
        in_specs=[pl.BlockSpec(memory_space=pltpu.SMEM), vmem],
        out_specs=(vmem, vmem),
        scratch_shapes=[pltpu.VMEM((TILES + 1, S, LANES), F32)] * 4,
        name="place",
    )(offsets, lists)


def fft8(values):
    half = math.sqrt(0.5)

    def add(a, b):
        return a[0] + b[0], a[1] + b[1]

    def sub(a, b):
        return a[0] - b[0], a[1] - b[1]

    def turn(a):
        return a[1], -a[0]

    def fft4(v):
        s0, d0 = add(v[0], v[2]), sub(v[0], v[2])
        s1, d1 = add(v[1], v[3]), turn(sub(v[1], v[3]))
        return add(s0, s1), add(d0, d1), sub(s0, s1), sub(d0, d1)

    even = fft4(values[0::2])
    odd = fft4(values[1::2])
    o1 = ((odd[1][0] + odd[1][1]) * half, (odd[1][1] - odd[1][0]) * half)
    o2 = turn(odd[2])
    o3 = ((odd[3][1] - odd[3][0]) * half, (odd[3][0] + odd[3][1]) * -half)
    odd = (odd[0], o1, o2, o3)
    return [add(e, o) for e, o in zip(even, odd)] + [sub(e, o) for e, o in zip(even, odd)]


def transform_kernel(flip, rows_ref, twist_ref, matrix_ref, *rest):
    out_ref, mid_ref, sec_ref = rest[-3:]
    for part in range(2):
        lo, hi = 8 * part, HALF + 8 * part
        for t2 in range(8):
            made = fft8(
                [
                    (
                        rows_ref[8 * t1 + t2, lo : lo + 8, :].astype(F32),
                        rows_ref[8 * t1 + t2, hi : hi + 8, :].astype(F32),
                    )
                    for t1 in range(8)
                ]
            )
            for q1 in range(8):
                re, im = made[q1]
                angle = -2 * math.pi * t2 * q1 / 64
                if t2 * q1:
                    c, s = math.cos(angle), math.sin(angle)
                    re, im = re * c - im * s, im * c + re * s
                mid_ref[0, q1 * 8 + t2] = re
                mid_ref[1, q1 * 8 + t2] = im
        for q1 in range(8):
            made = fft8([(mid_ref[0, q1 * 8 + t2], mid_ref[1, q1 * 8 + t2]) for t2 in range(8)])
            for q2 in range(8):
                at = (q1 + 8 * q2) * 8
                sec_ref[0, part, at : at + 8] = made[q2][0]
                sec_ref[1, part, at : at + 8] = made[q2][1]
    contract = (((1,), (1,)), ((), ()))
    high = matrix_ref[0]
    low = matrix_ref[1]
    for r in range(HALF):
        part, i = r // 8, r % 8
        sr = sec_ref[0, part, pl.ds(i, TILES, stride=8), :]
        si = sec_ref[1, part, pl.ds(i, TILES, stride=8), :]
        zr, zi = [], []
        for k in range(2):
            tr = twist_ref[0, k * TILES : (k + 1) * TILES]
            ti = twist_ref[1, k * TILES : (k + 1) * TILES]
            zr.append(sr * tr - si * ti)
            zi.append(si * tr + sr * ti)
        full = jnp.concatenate([jnp.concatenate(zr, 0), jnp.concatenate(zi, 0)], 1)
        top = full.astype(BF16)
        rest_ = (full - top.astype(F32)).astype(BF16)
        made = (
            lax.dot_general(high, top, contract, preferred_element_type=F32)
            + lax.dot_general(low, top, contract, preferred_element_type=F32)
            + lax.dot_general(high, rest_, contract, preferred_element_type=F32)
        )
        place_at = HALF - 1 - r if flip else r
        part, i = place_at // 8, place_at % 8
        out_ref[0, part, pl.ds(i, TILES, stride=8), :] = made[:TILES]
        out_ref[1, part, pl.ds(i, TILES, stride=8), :] = made[TILES:]


def tables(flip):
    shift = 1 if flip else 0
    k = np.arange(LANES)[:, None]
    n = np.arange(LANES)[None, :] + shift
    angle = -2 * np.pi * ((k * n) % G) / G
    twist = np.stack([np.cos(angle), np.sin(angle)]) / math.sqrt(G * K)
    t = np.arange(TILES)[:, None]
    angle = 2 * np.pi * ((t * n) % TILES) / TILES
    c, s = np.cos(angle), np.sin(angle)
    sign = -1.0 if flip else 1.0
    matrix = np.concatenate([np.concatenate([c, s], 1), sign * np.concatenate([-s, c], 1)], 0)
    high = matrix.astype(BF16)
    low = (matrix - high.astype(np.float64)).astype(BF16)
    return twist.astype(np.float32), np.stack([high, low])


def transform(rows, flip, earlier=None):
    vmem = pl.BlockSpec(memory_space=pltpu.VMEM)
    where = 1 if flip else 0
    args = list(map(jnp.asarray, tables(flip)))
    specs = [vmem, vmem, vmem]
    if earlier is not None:
        args.append(earlier)
        specs.append(pl.BlockSpec(memory_space=pl.ANY))
    return pl.pallas_call(
        functools.partial(transform_kernel, flip),
        grid=(1,),
        out_shape=jax.ShapeDtypeStruct((2, 4, 8 * TILES, LANES), F32),
        in_specs=specs,
        out_specs=pl.BlockSpec((2, 2, 8 * TILES, LANES), lambda i: (0, where, 0, 0)),
        scratch_shapes=[
            pltpu.VMEM((2, TILES, 8, LANES), F32),
            pltpu.VMEM((2, 2, 8 * TILES, LANES), F32),
        ],
        input_output_aliases={} if earlier is None else {3: 0},
        cost_estimate=pl.CostEstimate(flops=600_000_000, bytes_accessed=4_000_000, transcendentals=0),
        name="transform_mirror" if flip else "transform_own",
    )(rows, *args)


def shards(visibilities, coordinates, block_index, counts, col_offset):
    lists = make_subgrids(visibilities[0], coordinates[0], block_index, counts)
    firsts = jnp.stack([col_offset, G - S - col_offset]).reshape(2, S, 1, CAP)
    firsts = jnp.pad(firsts, ((0, 0), (0, 0), (0, 0), (0, LANES - CAP)))
    lists, firsts = exchange(lists, firsts)
    own, low = place(firsts, lists)
    total = lax.axis_size("band") * lax.axis_size("wgrp")
    other = lax.ppermute(low, ("band", "wgrp"), [(i, total - 1 - i) for i in range(total)])
    out = transform(own, False)
    out = transform(other, True, out)
    out = out.reshape(2, 4, TILES, 8, LANES)
    return jnp.transpose(out, (0, 1, 3, 2, 4)).reshape(1, 2, S, G)


def solution(mesh):
    placed = (
        P("wgrp", "band", None),
        P("wgrp", "band", None),
        P("wgrp", "band"),
        P("wgrp", "band"),
        P("wgrp", "band"),
    )
    return jax.shard_map(
        shards, mesh=mesh, in_specs=placed, out_specs=P("wgrp", None, "band", None), check_vma=False
    )
```

time: 816 us -> 108 us (0.13); the launches traced: 807 us -> 108 us
  matrix products: 249 us -> 0 us
  local copies, waits for them, and re-layouts: 230 us -> 2.08 us
  blocking collectives: 143 us -> 0 us
  Pallas kernels: 0 us -> 78 us
  other arithmetic: 74.1 us -> 1.39 us
  waiting for transfers between devices: 73.1 us -> 20.9 us
  starting transfers between devices: 28.4 us -> 5.21 us
  loops' own time: 9.47 us -> 0 us
    dot_general x24 -> x0, matrix products: 249 us -> none  [the longest x16 236 us: product(): jnp.einsum('nyk,nxk->nyx', left, right, preferred_element_type=jnp.float32)]
    all_to_all x3 -> x0, blocking collectives: 143 us -> none  [the longest x1 54.3 us: shards(): lax.all_to_all(spread, 'band', split_axis=2, concat_axis=3, tiled=True)]
    pallas_call x0 -> x5, Pallas kernels: none -> 78 us  [the longest x1 42.5 us: exchange(): pl.pallas_call(exchange_kernel, out_shape=(jax.ShapeDtypeStruct(lists.sha...]
    all_to_all x3 -> x0, waiting for transfers between devices: 73.1 us -> none  [the longest x1 46.9 us: shards(): lax.all_to_all(computed, 'band', split_axis=0, concat_axis=0, tiled=True)]
    slice x7 -> x0, local copies, waits for them, and re-layouts: 58.9 us -> none  [the longest x2 33.6 us: shards(): mirrored[:, 1]]
    scatter-add x1 -> x0, other arithmetic: 46.5 us -> none  [shards(): placed = jnp.zeros((G, 2 * S), jnp.float32).at[columns].add(values)]
    all_to_all x9 -> x0, local copies, waits for them, and re-layouts: 44.4 us -> none  [the longest x2 19.3 us: shards(): lax.all_to_all(spread, 'band', split_axis=2, concat_axis=3, tiled=True)]
    unnamed x15 -> x3, local copies, waits for them, and re-layouts: 35.5 us -> 1.3 us
  transfers between devices with their start and end apart: 3 -> 1, of which waited for: 2 -> 1; matrix products, arithmetic and copies ran while one was open for 32% -> 0% of each run, Pallas kernels for 0% -> 3%
where the time goes in v1:
time: 108 us
  Pallas kernels  78 us (72%)
  waiting for transfers between devices  20.9 us (19%)
  starting transfers between devices  5.21 us (5%)
  local copies, waits for them, and re-layouts  2.08 us (2%)
  other arithmetic  1.39 us (1%)
    pallas_call x1, Pallas kernels, exchange(): pl.pallas_call(exchange_kernel, out_shape=(jax.ShapeDtypeStruct(lists.sha...  42.5 us
    ppermute x1, waiting for transfers between devices, shards(): lax.ppermute(low, ('band', 'wgrp'), [(i, total - 1 - i) for i in range(to...  20.9 us
    pallas_call x1, Pallas kernels, place(): pl.pallas_call(place_kernel, out_shape=(jax.ShapeDtypeStruct((TILES, S, L...  14.8 us
    pallas_call x1, Pallas kernels, make_subgrids(): pl.pallas_call(subgrid_kernel, out_shape=jax.ShapeDtypeStruct((2, S, 2, S...  13.4 us
    pallas_call x2, Pallas kernels, transform(): pl.pallas_call(functools.partial(transform_kernel, flip), grid=(1,), out_...  7.31 us
    ppermute x1, starting transfers between devices, shards(): lax.ppermute(low, ('band', 'wgrp'), [(i, total - 1 - i) for i in range(to...  5.21 us
  transfers between devices with their start and end apart: 1, of which 1 were waited for; matrix products, arithmetic and copies ran while one was open for 0% of the time, Pallas kernels for 3%

profile of v1, /device:TPU:1, one launch (start us, length us, event | category | flops | bytes accessed | tf_op | source)
XLA Modules:
  0.0 107.6 jit_solution(9963946131426703877)
XLA Ops:
  0.0 0.5 broadcast.8
  0.5 1.3 %fusion = (s32[256]{0:T(256)S(1)}, s32[256]{0:T(256)S(1)}) fusion(s32[1,256]{1,0:T(1,128)} %param.13, s32[]{:T(128)} %broadcast.8), kind=kLoop, calls=%fused_computation.2 | loop fusion | flops 256 | bytes 3076 | tf_op args[4]
  1.9 0.1 stack.9
  1.9 0.1 stack.10
  2.1 0.6 pad.4.offs_ref
  2.7 13.4 %subgrids.1.send_ref = bf16[2,32,2,32,128]{4,3,2,1,0:T(8,128)(2,1)} custom-call(s32[1,256]{1,0:T(1,128)} %index_ref.1, s32[1,32]{1,0:T(1,128)} %counts_ref.1, bf16[64,512]{1,0:T(8,128)(2,1)} %bitcast.9, bf16[64,512]{1,0:T(8,128)(2,1)} %bitcast.10), custom_call_target="tpu_custom_call" | custom-call | tf_op jit(solution)/shard_map/subgrids/pallas_call | solution.py:133
  16.1 42.5 %exchange.1 = (bf16[2,32,2,32,128]{4,3,2,1,0:T(8,128)(2,1)}, s32[2,32,1,128]{3,2,1,0:T(1,128)}) custom-call(bf16[2,32,2,32,128]{4,3,2,1,0:T(8,128)(2,1)} %subgrids.1.send_ref, s32[2,32,1,128]{3,2,1,0:T(1,128)} %pad.4.offs_ref), custom_call_target="tpu_custom_call" | custom-call | tf_op jit(solution)/shard_map/exchange/pallas_call | solution.py:229
  58.6 14.8 %place.1 = (f32[64,32,128]{2,1,0:T(8,128)}, bf16[64,32,128]{2,1,0:T(8,128)(2,1)}) custom-call(s32[2,32,1,128]{3,2,1,0:T(1,128)} %get-tuple-element.9.offs_ref, bf16[2,32,2,32,128]{4,3,2,1,0:T(8,128)(2,1)} %get-tuple-element.10.lists_ref), custom_call_target="tpu_custom_call" | custom-call | tf_op jit(solution)/shard_map/place/pallas_call | solution.py:281
  73.4 5.2 %collective-permute-start = (bf16[64,32,128]{2,1,0:T(8,128)(2,1)}, bf16[64,32,128]{2,1,0:T(8,128)(2,1)S(1)}, u32[]{:S(2)}, u32[]{:S(2)}) collective-permute-start(bf16[64,32,128]{2,1,0:T(8,128)(2,1)} %get-tuple-element.11), channel_id=1, source_target_pairs={{0,255},{1,254},{2,253},{3,252},{4,251},{5,250},{6,249},{7,248},{8... | collective-permute-start | bytes 1572872 | tf_op jit(solution)/shard_map/ppermute | solution.py:422
  78.6 3.7 %transform_own.1.rest_0_ = f32[2,4,512,128]{3,2,1,0:T(8,128)} custom-call(f32[64,32,128]{2,1,0:T(8,128)} %get-tuple-element.12.rows_ref, f32[2,128,128]{2,1,0:T(8,128)} %constant.12.clone.twist_ref, bf16[2,128,256]{2,1,0:T(8,128)(2,1)} %constant.13.clone.matrix_ref), custom_call_target="tpu_custom_call" | custom-call | flops 600000000 | bytes 4000000 | tf_op jit(solution)/shard_map/transform_own/pallas_call | solution.py:399
  82.4 20.9 %collective-permute-done.rows_ref = bf16[64,32,128]{2,1,0:T(8,128)(2,1)S(1)} collective-permute-done((bf16[64,32,128]{2,1,0:T(8,128)(2,1)}, bf16[64,32,128]{2,1,0:T(8,128)(2,1)S(1)}, u32[]{:S(2)}, u32[]{:S(2)}) %collective-permute-start) | collective-permute-done | bytes 524320 | tf_op jit(solution)/shard_map/ppermute | solution.py:422
  103.3 0.0 copy-start
  103.3 0.8 copy-done
  104.1 3.6 %transform_mirror.1 = f32[2,4,512,128]{3,2,1,0:T(8,128)} custom-call(bf16[64,32,128]{2,1,0:T(8,128)(2,1)} %copy-done, f32[2,128,128]{2,1,0:T(8,128)} %constant.14.clone.twist_ref, bf16[2,128,256]{2,1,0:T(8,128)(2,1)} %constant.15.clone.matrix_ref, f32[2,4,512,128]{3,2,1,0:T(8,128)} %transform_own.1.rest_0_), custom_call_target="tpu_custom_call", output_to_operand_aliasing={{}: (3, {})} | custom-call | flops 600000000 | bytes 4000000 | tf_op jit(solution)/shard_map/transform_mirror/pallas_call | solution.py:399
  (1 shorter events, 0.0 us)
Async XLA Ops:
  73.4 29.8 %collective-permute-start = (bf16[64,32,128]{2,1,0:T(8,128)(2,1)}, bf16[64,32,128]{2,1,0:T(8,128)(2,1)S(1)}, u32[]{:S(2)}, u32[]{:S(2)}) collective-permute-start(bf16[64,32,128]{2,1,0:T(8,128)(2,1)} %get-tuple-element.11), channel_id=1, source_target_pairs={{0,255},{1,254},{2,253},{3,252},{4,251},{5,250},{6,249},{7,248},{8... | collective-permute-start | bytes 1572872 | tf_op jit(solution)/shard_map/ppermute | solution.py:422
  103.3 0.8 copy-start

commit v2 on v1

v2 whole, which is shorter than its diff:
```python
import functools
import math

import jax
import jax.numpy as jnp
import numpy as np
from jax import lax
from jax.experimental import pallas as pl
from jax.experimental.pallas import tpu as pltpu
from jax.sharding import PartitionSpec as P

S = 32
G = 8192
K = 256
CAP = 8
NBLK = 64
LANES = 128
TILES = G // LANES
HALF = S // 2
MESH = pl.DeviceIdType.MESH
F32 = jnp.float32
BF16 = jnp.bfloat16


def fit(func, degree):
    nodes = 0.125 + 0.125 * np.cos(np.pi * (np.arange(400) + 0.5) / 400)
    series = np.polynomial.chebyshev.Chebyshev.fit(nodes, func(nodes), degree, domain=[0, 0.25])
    return [float(c) for c in series.convert(kind=np.polynomial.Polynomial).coef]


SIN_COEF = fit(lambda q: np.sin(2 * np.pi * np.sqrt(q)) / np.sqrt(q), 6)
COS_COEF = fit(lambda q: np.cos(2 * np.pi * np.sqrt(q)), 7)


def horner(coef, q):
    total = jnp.full_like(q, coef[-1])
    for c in coef[-2::-1]:
        total = total * q + c
    return total


def unit(cycles):
    frac = cycles - jnp.floor(cycles + 0.5)
    q = frac * frac
    return horner(COS_COEF, q), frac * horner(SIN_COEF, q)


def cmul(a, b):
    return a[0] * b[0] - a[1] * b[1], a[0] * b[1] + a[1] * b[0]


def spread(index_ref, counts_ref, vis_ref, coord_ref, offs_ref, recv_ref, roff_ref, *scratch):
    vf_ref, z_ref, sub_ref, send_ref, send_sem, recv_sem, osend_sem, orecv_sem, own_sem = scratch
    band = lax.axis_index("band")
    plane = lax.axis_index("wgrp")
    z = band // 4
    x = band % 4

    def target(j):
        turn = j // 4
        dz = 4 + ((turn + 1) // 2) * (2 * (turn % 2) - 1)
        dx = 3 - j % 4
        return ((z + dz) % 8) * 4 + (x + dx) % 4

    def device(half, d):
        return (d + half * (31 - 2 * d), plane + half * (7 - 2 * plane))

    barrier = pltpu.get_barrier_semaphore()

    def greet(j, carry):
        pl.semaphore_signal(barrier, inc=1, device_id=device(0, target(j)), device_id_type=MESH)
        pl.semaphore_signal(barrier, inc=1, device_id=device(1, target(j)), device_id_type=MESH)
        return carry

    lax.fori_loop(0, S - 1, greet, 0)
    pl.semaphore_signal(barrier, inc=1, device_id=device(1, band), device_id_type=MESH)

    vf_ref[...] = vis_ref[...].astype(F32)
    for axis in range(2):
        step = unit(coord_ref[:, axis * K : (axis + 1) * K].astype(F32) * (1.0 / S))
        for which in range(5):
            z_ref[axis, which, 0] = step[0]
            z_ref[axis, which, 1] = step[1]
            if which < 4:
                step = ((step[0] - step[1]) * (step[0] + step[1]), 2.0 * (step[0] * step[1]))
    sub_ref[:, NBLK] = jnp.zeros((2, S, LANES), BF16)
    sublane = lax.broadcasted_iota(jnp.int32, (8, K), 0)
    bits = [(sublane & bit) != 0 for bit in (1, 2, 4)]
    first = sublane == 0

    def one_block(m):
        row = pl.ds(m, 1)

        def power(axis, which):
            return z_ref[axis, which, 0, row, :], z_ref[axis, which, 1, row, :]

        def low_powers(axis):
            factors = []
            for which, bit in enumerate(bits):
                re, im = power(axis, which)
                factors.append((jnp.where(bit, re, 1.0), jnp.where(bit, im, 0.0)))
            return cmul(cmul(factors[0], factors[1]), factors[2])

        base = low_powers(0)
        z8 = power(0, 3)
        z16 = power(0, 4)
        rr, ii, ri, ir = z8[0] * base[0], z8[1] * base[1], z8[0] * base[1], z8[1] * base[0]
        low = (z16[0] * base[0] + z16[1] * base[1], z16[0] * base[1] - z16[1] * base[0])
        parts = (low, (rr + ii, ri - ir), base, (rr - ii, ri + ir))
        a, b = vf_ref[row, 0:K], vf_ref[row, K : 2 * K]
        plain, turned = [], []
        for i, (re, im) in enumerate(parts):
            ar, bi, ai, br = a * re, b * im, a * im, b * re
            plain.append((ar - bi, ai + br))
            if i == 0:
                re, im = jnp.where(first, z16[0], re), jnp.where(first, z16[1], im)
                ar, bi, ai, br = a * re, b * im, a * im, b * re
            turned.append((ar + bi, ai - br))
        right = jnp.concatenate(
            [
                jnp.concatenate([jnp.concatenate([c[i] for c in made], 0) for i in range(2)], 1).astype(BF16)
                for made in (plain, turned)
            ],
            0,
        )
        base = low_powers(1)
        z8 = power(1, 3)
        z16 = power(1, 4)
        pair = (cmul((z16[0], -z16[1]), base), cmul((z8[0], -z8[1]), base))
        step = power(1, 0)
        rows = []
        for table in (pair, tuple(cmul(step, p) for p in pair)):
            cos = jnp.concatenate([p[0] for p in table], 0)
            sin = jnp.concatenate([p[1] for p in table], 0)
            rows.append(jnp.concatenate([cos, -sin], 1))
            rows.append(jnp.concatenate([sin, cos], 1))
        left = jnp.concatenate(rows, 0).astype(BF16)
        made = lax.dot_general(left, right, (((1,), (1,)), ((), ())), preferred_element_type=F32)
        for half in range(2):
            piece = made[half * S : (half + 1) * S, half * S : (half + 1) * S]
            piece = jnp.concatenate([piece] * 4, 1)
            if half:
                piece = pltpu.roll(piece, LANES - 1, 1)
            sub_ref[half, m] = piece.astype(BF16)

    def some_blocks(i, carry):
        for j in range(4):
            one_block(i * 4 + j)
        return carry

    lax.fori_loop(0, NBLK // 4, some_blocks, 0)
    lane = lax.broadcasted_iota(jnp.int32, (S, LANES), 1) // S

    def expand(j):
        d = target(j)
        live = counts_ref[0, d]
        for group in range(2):
            idx = []
            for i in range(4):
                slot = group * 4 + i
                idx.append(jnp.where(slot < live, index_ref[0, d * CAP + slot], NBLK))
            for half in range(2):
                value = sub_ref[half, idx[3]]
                for i in range(3):
                    value = jnp.where(lane == i, sub_ref[half, idx[i]], value)
                send_ref[half, d, group] = value

    def copies(half, j):
        d = target(j)
        data = pltpu.make_async_remote_copy(
            src_ref=send_ref.at[half, d],
            dst_ref=recv_ref.at[half, band],
            send_sem=send_sem.at[half],
            recv_sem=recv_sem.at[half],
            device_id=device(half, d),
            device_id_type=MESH,
        )
        offs = pltpu.make_async_remote_copy(
            src_ref=offs_ref.at[d // 16],
            dst_ref=roff_ref.at[half, band],
            send_sem=osend_sem.at[half],
            recv_sem=orecv_sem.at[half],
            device_id=device(half, d),
            device_id_type=MESH,
        )
        return data, offs

    def send(half, j):
        for copy in copies(half, j):
            copy.start()

    expand(0)
    pl.semaphore_wait(barrier, 2 * S - 1)

    def pass_on(j, carry):
        expand(j)
        send(0, j - 1)
        send(1, j - 1)
        return carry

    lax.fori_loop(1, S, pass_on, 0)
    own_offs = pltpu.make_async_copy(offs_ref.at[band // 16], roff_ref.at[0, band], own_sem.at[1])
    own_offs.start()
    send(1, S - 1)
    own = pltpu.make_async_copy(send_ref.at[0, band], recv_ref.at[0, band], own_sem.at[0])
    own.start()
    own_offs.wait()
    own.wait()
    for half, count in ((0, S - 1), (1, S)):
        for arrived, left_sem, come_sem in ((roff_ref, osend_sem, orecv_sem), (recv_ref, send_sem, recv_sem)):
            everything = arrived.at[half, 0:count]
            both = pltpu.make_async_remote_copy(
                src_ref=everything,
                dst_ref=everything,
                send_sem=left_sem.at[half],
                recv_sem=come_sem.at[half],
                device_id=device(1, band),
                device_id_type=MESH,
            )
            both.wait_send()
            both.wait_recv()


def spread_lists(vis, coord, index, counts, offsets):
    anywhere = pl.BlockSpec(memory_space=pl.ANY)
    vmem = pl.BlockSpec(memory_space=pltpu.VMEM)
    smem = pl.BlockSpec(memory_space=pltpu.SMEM)
    return pl.pallas_call(
        spread,
        out_shape=(
            jax.ShapeDtypeStruct((2, S, 2, S, LANES), BF16),
            jax.ShapeDtypeStruct((2, S, 1, LANES), jnp.int32),
        ),
        in_specs=[smem, smem, vmem, vmem, anywhere],
        out_specs=(anywhere, anywhere),
        scratch_shapes=[
            pltpu.VMEM((NBLK, 2 * K), F32),
            pltpu.VMEM((2, 5, 2, NBLK, K), F32),
            pltpu.VMEM((2, NBLK + 1, S, LANES), BF16),
            pltpu.VMEM((2, S, 2, S, LANES), BF16),
        ]
        + [pltpu.SemaphoreType.DMA((2,))] * 5,
        compiler_params=pltpu.CompilerParams(collective_id=0, has_side_effects=True),
        name="spread",
    )(index, counts, vis, coord, offsets)


def place_kernel(offs_ref, lists_ref, out_ref, low_ref, *slabs):
    zero = jnp.zeros((8, LANES), F32)
    band = lax.axis_index("band")

    def clear(t, carry):
        for slab in slabs:
            slab[t] = jnp.zeros((S, LANES), F32)
        return carry

    lax.fori_loop(0, TILES + 1, clear, 0)
    lane = lax.broadcasted_iota(jnp.int32, (8, LANES), 1)

    for half in range(2):
        base = ((31 - band if half else band) & 15) * CAP

        def place(i, carry, half=half, base=base):
            for group in range(2):
                values = lists_ref[half, i, group].astype(F32)
                for j, slab in enumerate(slabs):
                    start = offs_ref[half, i, 0, base + (group * 4 + j)]
                    if half:
                        start = G - S - start
                    tile = lax.shift_right_logical(start, 7)
                    first = start & (LANES - 1)
                    turned = pltpu.roll(values, (first - S * j) & (LANES - 1), 1)
                    inner = (lane >= first) & (lane < first + S)
                    outer = lane < first + (S - LANES)
                    for p in range(0, S, 8):
                        slab[tile, p : p + 8] += jnp.where(inner, turned[p : p + 8], zero)
                        slab[tile + 1, p : p + 8] += jnp.where(outer, turned[p : p + 8], zero)
            return carry

        lax.fori_loop(0, S, place, 0, unroll=4)

    def gather(t, carry):
        total = (slabs[0][t] + slabs[1][t]) + (slabs[2][t] + slabs[3][t])
        out_ref[t] = total
        low_ref[t] = total.astype(BF16)
        return carry

    lax.fori_loop(0, TILES, gather, 0)


def place(offsets, lists):
    vmem = pl.BlockSpec(memory_space=pltpu.VMEM)
    return pl.pallas_call(
        place_kernel,
        out_shape=(
            jax.ShapeDtypeStruct((TILES, S, LANES), F32),
            jax.ShapeDtypeStruct((TILES, S, LANES), BF16),
        ),
        in_specs=[pl.BlockSpec(memory_space=pltpu.SMEM), vmem],
        out_specs=(vmem, vmem),
        scratch_shapes=[pltpu.VMEM((TILES + 1, S, LANES), F32)] * 4,
        name="place",
    )(offsets, lists)


def fft8(values):
    half = math.sqrt(0.5)

    def add(a, b):
        return a[0] + b[0], a[1] + b[1]

    def sub(a, b):
        return a[0] - b[0], a[1] - b[1]

    def turn(a):
        return a[1], -a[0]

    def fft4(v):
        s0, d0 = add(v[0], v[2]), sub(v[0], v[2])
        s1, d1 = add(v[1], v[3]), turn(sub(v[1], v[3]))
        return add(s0, s1), add(d0, d1), sub(s0, s1), sub(d0, d1)

    even = fft4(values[0::2])
    odd = fft4(values[1::2])
    o1 = ((odd[1][0] + odd[1][1]) * half, (odd[1][1] - odd[1][0]) * half)
    o2 = turn(odd[2])
    o3 = ((odd[3][1] - odd[3][0]) * half, (odd[3][0] + odd[3][1]) * -half)
    odd = (odd[0], o1, o2, o3)
    return [add(e, o) for e, o in zip(even, odd)] + [sub(e, o) for e, o in zip(even, odd)]


def transform_kernel(flip, rows_ref, twist_ref, matrix_ref, *rest):
    out_ref, mid_ref, sec_ref = rest[-3:]
    for part in range(2):
        lo, hi = 8 * part, HALF + 8 * part
        for t2 in range(8):
            made = fft8(
                [
                    (
                        rows_ref[8 * t1 + t2, lo : lo + 8, :].astype(F32),
                        rows_ref[8 * t1 + t2, hi : hi + 8, :].astype(F32),
                    )
                    for t1 in range(8)
                ]
            )
            for q1 in range(8):
                re, im = made[q1]
                angle = -2 * math.pi * t2 * q1 / 64
                if t2 * q1:
                    c, s = math.cos(angle), math.sin(angle)
                    re, im = re * c - im * s, im * c + re * s
                mid_ref[0, q1 * 8 + t2] = re
                mid_ref[1, q1 * 8 + t2] = im
        for q1 in range(8):
            made = fft8([(mid_ref[0, q1 * 8 + t2], mid_ref[1, q1 * 8 + t2]) for t2 in range(8)])
            for q2 in range(8):
                at = (q1 + 8 * q2) * 8
                sec_ref[0, part, at : at + 8] = made[q2][0]
                sec_ref[1, part, at : at + 8] = made[q2][1]
    contract = (((1,), (1,)), ((), ()))
    high = matrix_ref[0]
    low = matrix_ref[1]
    for r in range(HALF):
        part, i = r // 8, r % 8
        sr = sec_ref[0, part, pl.ds(i, TILES, stride=8), :]
        si = sec_ref[1, part, pl.ds(i, TILES, stride=8), :]
        zr, zi = [], []
        for k in range(2):
            tr = twist_ref[0, k * TILES : (k + 1) * TILES]
            ti = twist_ref[1, k * TILES : (k + 1) * TILES]
            zr.append(sr * tr - si * ti)
            zi.append(si * tr + sr * ti)
        full = jnp.concatenate([jnp.concatenate(zr, 0), jnp.concatenate(zi, 0)], 1)
        top = full.astype(BF16)
        rest_ = (full - top.astype(F32)).astype(BF16)
        made = (
            lax.dot_general(high, top, contract, preferred_element_type=F32)
            + lax.dot_general(low, top, contract, preferred_element_type=F32)
            + lax.dot_general(high, rest_, contract, preferred_element_type=F32)
        )
        place_at = HALF - 1 - r if flip else r
        part, i = place_at // 8, place_at % 8
        out_ref[0, part, pl.ds(i, TILES, stride=8), :] = made[:TILES]
        out_ref[1, part, pl.ds(i, TILES, stride=8), :] = made[TILES:]


def tables(flip):
    shift = 1 if flip else 0
    k = np.arange(LANES)[:, None]
    n = np.arange(LANES)[None, :] + shift
    angle = -2 * np.pi * ((k * n) % G) / G
    twist = np.stack([np.cos(angle), np.sin(angle)]) / math.sqrt(G * K)
    t = np.arange(TILES)[:, None]
    angle = 2 * np.pi * ((t * n) % TILES) / TILES
    c, s = np.cos(angle), np.sin(angle)
    sign = -1.0 if flip else 1.0
    matrix = np.concatenate([np.concatenate([c, s], 1), sign * np.concatenate([-s, c], 1)], 0)
    high = matrix.astype(BF16)
    low = (matrix - high.astype(np.float64)).astype(BF16)
    return twist.astype(np.float32), np.stack([high, low])


def transform(rows, flip, earlier=None):
    vmem = pl.BlockSpec(memory_space=pltpu.VMEM)
    where = 1 if flip else 0
    args = list(map(jnp.asarray, tables(flip)))
    specs = [vmem, vmem, vmem]
    if earlier is not None:
        args.append(earlier)
        specs.append(pl.BlockSpec(memory_space=pl.ANY))
    return pl.pallas_call(
        functools.partial(transform_kernel, flip),
        grid=(1,),
        out_shape=jax.ShapeDtypeStruct((2, 4, 8 * TILES, LANES), F32),
        in_specs=specs,
        out_specs=pl.BlockSpec((2, 2, 8 * TILES, LANES), lambda i: (0, where, 0, 0)),
        scratch_shapes=[
            pltpu.VMEM((2, TILES, 8, LANES), F32),
            pltpu.VMEM((2, 2, 8 * TILES, LANES), F32),
        ],
        input_output_aliases={} if earlier is None else {3: 0},
        cost_estimate=pl.CostEstimate(flops=600_000_000, bytes_accessed=4_000_000, transcendentals=0),
        name="transform_mirror" if flip else "transform_own",
    )(rows, *args)


def shards(visibilities, coordinates, block_index, counts, col_offset):
    lists, firsts = spread_lists(
        visibilities[0], coordinates[0], block_index, counts, col_offset.reshape(2, 1, LANES)
    )
    own, low = place(firsts, lists)
    total = lax.axis_size("band") * lax.axis_size("wgrp")
    other = lax.ppermute(low, ("band", "wgrp"), [(i, total - 1 - i) for i in range(total)])
    out = transform(own, False)
    out = transform(other, True, out)
    out = out.reshape(2, 4, TILES, 8, LANES)
    return jnp.transpose(out, (0, 1, 3, 2, 4)).reshape(1, 2, S, G)


def solution(mesh):
    placed = (
        P("wgrp", "band", None),
        P("wgrp", "band", None),
        P("wgrp", "band"),
        P("wgrp", "band"),
        P("wgrp", "band"),
    )
    return jax.shard_map(
        shards, mesh=mesh, in_specs=placed, out_specs=P("wgrp", None, "band", None), check_vma=False
    )
```

time: 108 us -> 86.4 us (0.80)
  Pallas kernels: 78 us -> 58.8 us
  waiting for transfers between devices: 20.9 us -> 25.9 us
  starting transfers between devices: 5.21 us -> 0.65 us
  other arithmetic: 1.39 us -> 0 us
  local copies, waits for them, and re-layouts: 2.08 us -> 0.79 us
    pallas_call x2 -> x1, Pallas kernels: 55.9 us -> 44.7 us  [spread_lists(): pl.pallas_call(spread, out_shape=(jax.ShapeDtypeStruct((2, S, 2, S, LANES...]
    pallas_call x1, Pallas kernels: 14.8 us -> 6.79 us  [place(): pl.pallas_call(place_kernel, out_shape=(jax.ShapeDtypeStruct((TILES, S, L...]
    ppermute x1, waiting for transfers between devices: 20.9 us -> 25.9 us  [shards(): lax.ppermute(low, ('band', 'wgrp'), [(i, total - 1 - i) for i in range(to...]
    ppermute x1, starting transfers between devices: 5.21 us -> 0.65 us  [shards(): lax.ppermute(low, ('band', 'wgrp'), [(i, total - 1 - i) for i in range(to...]
    unnamed x1 -> x0, other arithmetic: 1.34 us -> none
  transfers between devices with their start and end apart: 1 -> 1, of which waited for: 1 -> 1; matrix products, arithmetic and copies ran while one was open for 0% -> 0% of each run, Pallas kernels for 3% -> 4%
where the time goes in v2:
time: 86.4 us; the launch traced here: 86.2 us
  Pallas kernels  58.8 us (68%)
  waiting for transfers between devices  25.9 us (30%)
    pallas_call x1, Pallas kernels, spread_lists(): pl.pallas_call(spread, out_shape=(jax.ShapeDtypeStruct((2, S, 2, S, LANES...  44.7 us
    ppermute x1, waiting for transfers between devices, shards(): lax.ppermute(low, ('band', 'wgrp'), [(i, total - 1 - i) for i in range(to...  25.9 us
    pallas_call x2, Pallas kernels, transform(): pl.pallas_call(functools.partial(transform_kernel, flip), grid=(1,), out_...  7.31 us
    pallas_call x1, Pallas kernels, place(): pl.pallas_call(place_kernel, out_shape=(jax.ShapeDtypeStruct((TILES, S, L...  6.79 us
  transfers between devices with their start and end apart: 1, of which 1 were waited for; matrix products, arithmetic and copies ran while one was open for 0% of the time, Pallas kernels for 4%

profile of v2, /device:TPU:1, one launch (start us, length us, event | category | flops | bytes accessed | tf_op | source)
XLA Modules:
  0.0 86.2 jit_solution(18045443012370003217)
XLA Ops:
  0.0 44.7 %spread.1 = (bf16[2,32,2,32,128]{4,3,2,1,0:T(8,128)(2,1)}, s32[2,32,1,128]{3,2,1,0:T(1,128)}) custom-call(s32[1,256]{1,0:T(1,128)} %index_ref.1, s32[1,32]{1,0:T(1,128)} %counts_ref.1, bf16[64,512]{1,0:T(8,128)(2,1)} %bitcast.8, bf16[64,512]{1,0:T(8,128)(2,1)} %bitcast.9, s32[2,1,128]{2,1,0:T(1,128)} %bitcast.10), custom_call_target="tpu_custom_call" | custom-call | tf_op jit(solution)/shard_map/spread/pallas_call | solution.py:228
  44.7 6.8 %place.1 = (f32[64,32,128]{2,1,0:T(8,128)}, bf16[64,32,128]{2,1,0:T(8,128)(2,1)}) custom-call(s32[2,32,1,128]{3,2,1,0:T(1,128)} %get-tuple-element.9.offs_ref, bf16[2,32,2,32,128]{4,3,2,1,0:T(8,128)(2,1)} %get-tuple-element.10.lists_ref), custom_call_target="tpu_custom_call" | custom-call | tf_op jit(solution)/shard_map/place/pallas_call | solution.py:293
  51.5 0.6 collective-permute-start
  52.2 3.7 %transform_own.1.rest_0_ = f32[2,4,512,128]{3,2,1,0:T(8,128)} custom-call(f32[64,32,128]{2,1,0:T(8,128)} %get-tuple-element.12.rows_ref, f32[2,128,128]{2,1,0:T(8,128)} %constant.8.clone.twist_ref, bf16[2,128,256]{2,1,0:T(8,128)(2,1)} %constant.9.clone.matrix_ref), custom_call_target="tpu_custom_call" | custom-call | flops 600000000 | bytes 4000000 | tf_op jit(solution)/shard_map/transform_own/pallas_call | solution.py:411
  55.9 25.9 %collective-permute-done.rows_ref = bf16[64,32,128]{2,1,0:T(8,128)(2,1)S(1)} collective-permute-done((bf16[64,32,128]{2,1,0:T(8,128)(2,1)}, bf16[64,32,128]{2,1,0:T(8,128)(2,1)S(1)}, u32[]{:S(2)}, u32[]{:S(2)}) %collective-permute-start) | collective-permute-done | bytes 524320 | tf_op jit(solution)/shard_map/ppermute | solution.py:433
  81.8 0.0 copy-start
  81.8 0.8 copy-done
  82.6 3.6 %transform_mirror.1 = f32[2,4,512,128]{3,2,1,0:T(8,128)} custom-call(bf16[64,32,128]{2,1,0:T(8,128)(2,1)} %copy-done, f32[2,128,128]{2,1,0:T(8,128)} %constant.10.clone.twist_ref, bf16[2,128,256]{2,1,0:T(8,128)(2,1)} %constant.11.clone.matrix_ref, f32[2,4,512,128]{3,2,1,0:T(8,128)} %transform_own.1.rest_0_), custom_call_target="tpu_custom_call", output_to_operand_aliasing={{}: (3, {})} | custom-call | flops 600000000 | bytes 4000000 | tf_op jit(solution)/shard_map/transform_mirror/pallas_call | solution.py:411
Async XLA Ops:
  51.5 30.3 %collective-permute-start = (bf16[64,32,128]{2,1,0:T(8,128)(2,1)}, bf16[64,32,128]{2,1,0:T(8,128)(2,1)S(1)}, u32[]{:S(2)}, u32[]{:S(2)}) collective-permute-start(bf16[64,32,128]{2,1,0:T(8,128)(2,1)} %get-tuple-element.11), channel_id=1, source_target_pairs={{0,255},{1,254},{2,253},{3,252},{4,251},{5,250},{6,249},{7,248},{8... | collective-permute-start | bytes 1572872 | tf_op jit(solution)/shard_map/ppermute | solution.py:433
  81.8 0.8 copy-start

commit v3 on v2

v3 whole, which is shorter than its diff:
```python
import math

import jax
import jax.numpy as jnp
import numpy as np
from jax import lax
from jax.experimental import pallas as pl
from jax.experimental.pallas import tpu as pltpu
from jax.sharding import PartitionSpec as P

S = 32
G = 8192
K = 256
CAP = 8
NBLK = 64
LANES = 128
TILES = G // LANES
MESH = pl.DeviceIdType.MESH
F32 = jnp.float32
BF16 = jnp.bfloat16


def fit(func, degree):
    nodes = 0.125 + 0.125 * np.cos(np.pi * (np.arange(400) + 0.5) / 400)
    series = np.polynomial.chebyshev.Chebyshev.fit(nodes, func(nodes), degree, domain=[0, 0.25])
    return [float(c) for c in series.convert(kind=np.polynomial.Polynomial).coef]


SIN_COEF = fit(lambda q: np.sin(2 * np.pi * np.sqrt(q)) / np.sqrt(q), 6)
COS_COEF = fit(lambda q: np.cos(2 * np.pi * np.sqrt(q)), 7)


def horner(coef, q):
    total = jnp.full_like(q, coef[-1])
    for c in coef[-2::-1]:
        total = total * q + c
    return total


def unit(cycles):
    frac = cycles - jnp.floor(cycles + 0.5)
    q = frac * frac
    return horner(COS_COEF, q), frac * horner(SIN_COEF, q)


def cmul(a, b):
    return a[0] * b[0] - a[1] * b[1], a[0] * b[1] + a[1] * b[0]


def spread(index_ref, counts_ref, vis_ref, coord_ref, offs_ref, recv_ref, roff_ref, *scratch):
    vf_ref, z_ref, sub_ref, send_ref, data_ref, table_ref, number_ref = scratch[:7]
    send_sem, recv_sem, osend_sem, orecv_sem, own_sem, dsend_sem, drecv_sem, number_sem = scratch[7:]
    band = lax.axis_index("band")
    plane = lax.axis_index("wgrp")
    z = band // 4
    x = band % 4
    twin = ((z + 4) % 8) * 4 + x

    def target(j):
        return ((z + j // 4) % 8) * 4 + (x + j % 4) % 4

    def device(half, e):
        return (e, plane + half * (7 - 2 * plane))

    barrier = pltpu.get_barrier_semaphore()

    def greet(j, carry):
        pl.semaphore_signal(barrier, inc=1, device_id=device(0, target(j)), device_id_type=MESH)
        pl.semaphore_signal(barrier, inc=1, device_id=device(1, target(j)), device_id_type=MESH)
        return carry

    lax.fori_loop(1, S, greet, 0)
    pl.semaphore_signal(barrier, inc=1, device_id=device(1, band), device_id_type=MESH)

    table_ref[0, 0:2] = index_ref[...]
    table_ref[0, 2, :, 0:S] = counts_ref[...]
    numbers = pltpu.make_async_copy(table_ref.at[0], number_ref.at[0], number_sem.at[0])
    numbers.start()
    sub_ref[:, NBLK] = jnp.zeros((2, 2 * S, LANES), BF16)
    sublane = lax.broadcasted_iota(jnp.int32, (8, K), 0)
    bits = [(sublane & bit) != 0 for bit in (1, 2, 4)]
    first = sublane == 0
    lane = lax.broadcasted_iota(jnp.int32, (2 * S, LANES), 1) // S

    def prepare(vis, coord):
        vf_ref[...] = vis.astype(F32)
        for axis in range(2):
            step = unit(coord[:, axis * K : (axis + 1) * K].astype(F32) * (1.0 / S))
            for which in range(5):
                z_ref[axis, which, 0] = step[0]
                z_ref[axis, which, 1] = step[1]
                if which < 4:
                    step = ((step[0] - step[1]) * (step[0] + step[1]), 2.0 * (step[0] * step[1]))

    def one_block(m):
        row = pl.ds(m, 1)

        def power(axis, which):
            return z_ref[axis, which, 0, row, :], z_ref[axis, which, 1, row, :]

        def exponents(axis):
            factors = []
            for which, bit in enumerate(bits):
                re, im = power(axis, which)
                factors.append((jnp.where(bit, re, 1.0), jnp.where(bit, im, 0.0)))
            base = cmul(cmul(factors[0], factors[1]), factors[2])
            z8 = power(axis, 3)
            z16 = power(axis, 4)
            rr, ii, ri, ir = z8[0] * base[0], z8[1] * base[1], z8[0] * base[1], z8[1] * base[0]
            low = (z16[0] * base[0] + z16[1] * base[1], z16[0] * base[1] - z16[1] * base[0])
            return (low, (rr + ii, ri - ir), base, (rr - ii, ri + ir)), z16

        def instead(part, other):
            return jnp.where(first, other[0], part[0]), jnp.where(first, other[1], part[1])

        parts, z16 = exponents(0)
        a, b = vf_ref[row, 0:K], vf_ref[row, K : 2 * K]
        plain, turned = [], []
        for i, (re, im) in enumerate(parts):
            ar, bi, ai, br = a * re, b * im, a * im, b * re
            plain.append((ar - bi, ai + br))
            if i == 0:
                re, im = instead((re, im), z16)
                ar, bi, ai, br = a * re, b * im, a * im, b * re
            turned.append((ar + bi, ai - br))
        right = jnp.concatenate(
            [
                jnp.concatenate([jnp.concatenate([c[i] for c in made], 0) for i in range(2)], 1).astype(BF16)
                for made in (plain, turned)
            ],
            0,
        )
        parts, z16 = exponents(1)

        def rows(pair):
            cos = jnp.concatenate([p[0] for p in pair], 0)
            sin = jnp.concatenate([p[1] for p in pair], 0)
            return (
                jnp.concatenate([cos, -sin], 1).astype(BF16),
                jnp.concatenate([sin, cos], 1).astype(BF16),
            )

        begin, end = rows(parts[:2]), rows(parts[2:])
        other = rows((instead(parts[0], z16), parts[1]))
        left = jnp.concatenate(
            [begin[0], end[0], begin[1], end[1], other[0], end[0], other[1], end[1]], 0
        )
        made = lax.dot_general(left, right, (((1,), (1,)), ((), ())), preferred_element_type=F32)
        sub_ref[0, m] = jnp.concatenate([made[: 2 * S, :S]] * 4, 1).astype(BF16)
        piece = pltpu.roll(jnp.concatenate([made[2 * S :, S:]] * 4, 1), LANES - 1, 1)
        sub_ref[1, m] = jnp.concatenate(
            [pltpu.roll(piece[:S], S - 1, 0), pltpu.roll(piece[S:], S - 1, 0)], 0
        ).astype(BF16)

    def blocks(begin, end):
        def some_blocks(i, carry):
            for j in range(4):
                one_block(i * 4 + j)
            return carry

        lax.fori_loop(begin // 4, end // 4, some_blocks, 0)

    def served(half, q):
        dz = 2 - half - (q // 4 + 3 - half) % 4
        return ((z + dz + 8) % 8) * 4 + (x + 3 - q % 4) % 4

    def expand(which, q):
        for half in range(2):
            e = served(half, q)
            d = e + half * (31 - 2 * e)
            live = number_ref[which, 2, 0, d]
            for group in range(2):
                idx = []
                for i in range(4):
                    slot = group * 4 + i
                    idx.append(
                        jnp.where(slot < live, number_ref[which, d // 16, 0, (d % 16) * CAP + slot], NBLK)
                    )
                value = sub_ref[half, idx[3]]
                for i in range(3):
                    value = jnp.where(lane == i, sub_ref[half, idx[i]], value)
                send_ref[which, half, q, group] = value

    def send(which, half, q):
        pltpu.make_async_remote_copy(
            src_ref=send_ref.at[which, half, q],
            dst_ref=recv_ref.at[half, twin if which else band],
            send_sem=send_sem.at[half],
            recv_sem=recv_sem.at[half],
            device_id=device(half, served(half, q)),
            device_id_type=MESH,
        ).start()

    def send_lists(which):
        expand(which, 0)

        def pass_on(q, carry):
            expand(which, q)
            send(which, 0, q - 1)
            send(which, 1, q - 1)
            return carry

        lax.fori_loop(1, 16, pass_on, 0)

    def inputs():
        pairs = ((vis_ref, data_ref.at[0]), (coord_ref, data_ref.at[1]), (table_ref.at[0], table_ref.at[1]))
        return [
            pltpu.make_async_remote_copy(
                src_ref=src,
                dst_ref=dst,
                send_sem=dsend_sem.at[i],
                recv_sem=drecv_sem.at[i],
                device_id=device(0, twin),
                device_id_type=MESH,
            )
            for i, (src, dst) in enumerate(pairs)
        ]

    def offsets(half, e):
        d = e + half * (31 - 2 * e)
        return pltpu.make_async_remote_copy(
            src_ref=offs_ref.at[d // 16],
            dst_ref=roff_ref.at[half, band],
            send_sem=osend_sem.at[half],
            recv_sem=orecv_sem.at[half],
            device_id=device(half, e),
            device_id_type=MESH,
        )

    prepare(vis_ref[...], coord_ref[...])
    blocks(0, NBLK // 2)
    pl.semaphore_wait(barrier, 2 * S - 1)
    for copy in inputs():
        copy.start()
    blocks(NBLK // 2, NBLK)
    numbers.wait()
    own_offs = pltpu.make_async_copy(offs_ref.at[band // 16], roff_ref.at[0, band], own_sem.at[1])
    own_offs.start()
    send_lists(0)
    send(0, 1, 15)
    own = pltpu.make_async_copy(send_ref.at[0, 0, 15], recv_ref.at[0, band], own_sem.at[0])
    own.start()
    for copy in inputs():
        copy.wait()
    numbers = pltpu.make_async_copy(table_ref.at[1], number_ref.at[1], number_sem.at[1])
    numbers.start()
    prepare(data_ref[0], data_ref[1])
    blocks(0, NBLK)
    numbers.wait()
    send_lists(1)
    send(1, 1, 15)
    twins = pltpu.make_async_copy(send_ref.at[1, 0, 15], recv_ref.at[0, twin], own_sem.at[2])
    twins.start()

    def tell(j, carry):
        offsets(0, target(j)).start()
        offsets(1, target(j)).start()
        return carry

    lax.fori_loop(1, S, tell, 0)
    offsets(1, band).start()
    own_offs.wait()
    own.wait()
    twins.wait()
    for half in range(2):
        for arrived, local, left_sem, come_sem in (
            (roff_ref, 1, osend_sem, orecv_sem),
            (recv_ref, 2, send_sem, recv_sem),
        ):
            everything = arrived.at[half, 0 : S if half else S - local]
            both = pltpu.make_async_remote_copy(
                src_ref=everything,
                dst_ref=everything,
                send_sem=left_sem.at[half],
                recv_sem=come_sem.at[half],
                device_id=device(1, band),
                device_id_type=MESH,
            )
            both.wait_send()
            both.wait_recv()


def spread_lists(vis, coord, index, counts, offsets):
    anywhere = pl.BlockSpec(memory_space=pl.ANY)
    vmem = pl.BlockSpec(memory_space=pltpu.VMEM)
    pair = pltpu.SemaphoreType.DMA((2,))
    three = pltpu.SemaphoreType.DMA((3,))
    return pl.pallas_call(
        spread,
        out_shape=(
            jax.ShapeDtypeStruct((2, S, 2, 2 * S, LANES), BF16),
            jax.ShapeDtypeStruct((2, S, 1, LANES), jnp.int32),
        ),
        in_specs=[vmem, vmem, vmem, vmem, anywhere],
        out_specs=(anywhere, anywhere),
        scratch_shapes=[
            pltpu.VMEM((NBLK, 2 * K), F32),
            pltpu.VMEM((2, 5, 2, NBLK, K), F32),
            pltpu.VMEM((2, NBLK + 1, 2 * S, LANES), BF16),
            pltpu.VMEM((2, 2, 16, 2, 2 * S, LANES), BF16),
            pltpu.VMEM((2, NBLK, 2 * K), BF16),
            pltpu.VMEM((2, 3, 1, LANES), jnp.int32),
            pltpu.SMEM((2, 3, 1, LANES), jnp.int32),
            pair,
            pair,
            pair,
            pair,
            three,
            three,
            three,
            pair,
        ],
        compiler_params=pltpu.CompilerParams(collective_id=0, has_side_effects=True),
        name="spread",
    )(index, counts, vis, coord, offsets)


def fft8(values):
    half = math.sqrt(0.5)

    def add(a, b):
        return a[0] + b[0], a[1] + b[1]

    def sub(a, b):
        return a[0] - b[0], a[1] - b[1]

    def turn(a):
        return a[1], -a[0]

    def fft4(v):
        s0, d0 = add(v[0], v[2]), sub(v[0], v[2])
        s1, d1 = add(v[1], v[3]), turn(sub(v[1], v[3]))
        return add(s0, s1), add(d0, d1), sub(s0, s1), sub(d0, d1)

    even = fft4(values[0::2])
    odd = fft4(values[1::2])
    o1 = ((odd[1][0] + odd[1][1]) * half, (odd[1][1] - odd[1][0]) * half)
    o2 = turn(odd[2])
    o3 = ((odd[3][1] - odd[3][0]) * half, (odd[3][0] + odd[3][1]) * -half)
    odd = (odd[0], o1, o2, o3)
    return [add(e, o) for e, o in zip(even, odd)] + [sub(e, o) for e, o in zip(even, odd)]


def finish_kernel(offs_ref, lists_ref, twist_ref, matrix_ref, out_ref, mid_ref, sec_ref, *slabs):
    part = pl.program_id(0)

    @pl.when(part == 0)
    def _():
        band = lax.axis_index("band")
        zero = jnp.zeros((8, LANES), F32)

        def clear(t, carry):
            for slab in slabs:
                slab[t] = jnp.zeros((2 * S, LANES), F32)
            return carry

        lax.fori_loop(0, TILES + 1, clear, 0)
        lane = lax.broadcasted_iota(jnp.int32, (8, LANES), 1)
        for half in range(2):
            base = ((31 - band if half else band) & 15) * CAP

            def place(i, carry, half=half, base=base):
                for group in range(2):
                    values = lists_ref[half, i, group].astype(F32)
                    for j, slab in enumerate(slabs):
                        start = offs_ref[half, i, 0, base + (group * 4 + j)]
                        if half:
                            start = G - S - start
                        tile = lax.shift_right_logical(start, 7)
                        first = start & (LANES - 1)
                        turned = pltpu.roll(values, (first - S * j) & (LANES - 1), 1)
                        inner = (lane >= first) & (lane < first + S)
                        outer = lane < first + (S - LANES)
                        for p in range(0, 2 * S, 8):
                            slab[tile, p : p + 8] += jnp.where(inner, turned[p : p + 8], zero)
                            slab[tile + 1, p : p + 8] += jnp.where(outer, turned[p : p + 8], zero)
                return carry

            lax.fori_loop(0, S, place, 0, unroll=2)

    def folded(t, row):
        at = pl.ds(pl.multiple_of(row, 8), 8)
        return (slabs[0][t, at] + slabs[1][t, at]) + (slabs[2][t, at] + slabs[3][t, at])

    for t2 in range(8):
        made = fft8([(folded(8 * t1 + t2, 8 * part), folded(8 * t1 + t2, 8 * part + S)) for t1 in range(8)])
        for q1 in range(8):
            re, im = made[q1]
            angle = -2 * math.pi * t2 * q1 / 64
            if t2 * q1:
                c, s = math.cos(angle), math.sin(angle)
                re, im = re * c - im * s, im * c + re * s
            mid_ref[0, q1 * 8 + t2] = re
            mid_ref[1, q1 * 8 + t2] = im
    for q1 in range(8):
        made = fft8([(mid_ref[0, q1 * 8 + t2], mid_ref[1, q1 * 8 + t2]) for t2 in range(8)])
        for q2 in range(8):
            at = (q1 + 8 * q2) * 8
            sec_ref[0, at : at + 8] = made[q2][0]
            sec_ref[1, at : at + 8] = made[q2][1]
    matrix = matrix_ref[...]
    for r in range(8):
        sr = sec_ref[0, pl.ds(r, TILES, stride=8), :]
        si = sec_ref[1, pl.ds(r, TILES, stride=8), :]
        zr, zi = [], []
        for k in range(2):
            tr = twist_ref[0, k * TILES : (k + 1) * TILES]
            ti = twist_ref[1, k * TILES : (k + 1) * TILES]
            zr.append(sr * tr - si * ti)
            zi.append(si * tr + sr * ti)
        full = jnp.concatenate([jnp.concatenate(zr, 0), jnp.concatenate(zi, 0)], 1).astype(BF16)
        made = lax.dot_general(matrix, full, (((1,), (1,)), ((), ())), preferred_element_type=F32)
        made = made[:LANES] + made[LANES:]
        out_ref[0, 0, pl.ds(r, TILES, stride=8), :] = made[:TILES]
        out_ref[1, 0, pl.ds(r, TILES, stride=8), :] = made[TILES:]


def tables():
    k = np.arange(LANES)[:, None]
    n = np.arange(LANES)[None, :]
    angle = -2 * np.pi * ((k * n) % G) / G
    twist = np.stack([np.cos(angle), np.sin(angle)]) / math.sqrt(G * K)
    t = np.arange(TILES)[:, None]
    angle = 2 * np.pi * ((t * n) % TILES) / TILES
    c, s = np.cos(angle), np.sin(angle)
    matrix = np.concatenate([np.concatenate([c, s], 1), np.concatenate([-s, c], 1)], 0)
    high = matrix.astype(BF16)
    low = (matrix - high.astype(np.float64)).astype(BF16)
    return twist.astype(np.float32), np.concatenate([high, low], 0)


def finish(offsets, lists):
    vmem = pl.BlockSpec(memory_space=pltpu.VMEM)
    return pl.pallas_call(
        finish_kernel,
        grid=(4,),
        out_shape=jax.ShapeDtypeStruct((2, 4, 8 * TILES, LANES), F32),
        in_specs=[pl.BlockSpec(memory_space=pltpu.SMEM), vmem, vmem, vmem],
        out_specs=pl.BlockSpec((2, 1, 8 * TILES, LANES), lambda i: (0, i, 0, 0)),
        scratch_shapes=[
            pltpu.VMEM((2, TILES, 8, LANES), F32),
            pltpu.VMEM((2, 8 * TILES, LANES), F32),
        ]
        + [pltpu.VMEM((TILES + 1, 2 * S, LANES), F32)] * 4,
        name="finish",
    )(offsets, lists, *map(jnp.asarray, tables()))


def shards(visibilities, coordinates, block_index, counts, col_offset):
    lists, firsts = spread_lists(
        visibilities[0],
        coordinates[0],
        block_index.reshape(2, 1, LANES),
        counts,
        col_offset.reshape(2, 1, LANES),
    )
    out = finish(firsts, lists)
    out = out.reshape(2, 4, TILES, 8, LANES)
    return jnp.transpose(out, (0, 1, 3, 2, 4)).reshape(1, 2, S, G)


def solution(mesh):
    placed = (
        P("wgrp", "band", None),
        P("wgrp", "band", None),
        P("wgrp", "band"),
        P("wgrp", "band"),
        P("wgrp", "band"),
    )
    return jax.shard_map(
        shards, mesh=mesh, in_specs=placed, out_specs=P("wgrp", None, "band", None), check_vma=False
    )
```

time: 86.4 us -> 62.9 us (0.73)
  waiting for transfers between devices: 25.9 us -> 0 us
  Pallas kernels: 58.8 us -> 62.7 us
    ppermute x1 -> x0, waiting for transfers between devices: 25.9 us -> none  [shards(): lax.ppermute(low, ('band', 'wgrp'), [(i, total - 1 - i) for i in range(to...]
    pallas_call x4 -> x2, Pallas kernels: 58.8 us -> 62.7 us  [the longest x1 50.6 us: spread_lists(): pl.pallas_call(spread, out_shape=(jax.ShapeDtypeStruct((2, S, 2, 2 * S, L...]
  transfers between devices with their start and end apart: 1 -> 0, of which waited for: 1 -> 0; matrix products, arithmetic and copies ran while one was open for 0% -> 0% of each run, Pallas kernels for 4% -> 0%
where the time goes in v3:
time: 62.9 us; the launch traced here: 62.7 us
  Pallas kernels  62.7 us (100%)
    pallas_call x1, Pallas kernels, spread_lists(): pl.pallas_call(spread, out_shape=(jax.ShapeDtypeStruct((2, S, 2, 2 * S, L...  50.6 us
    pallas_call x1, Pallas kernels, finish(): pl.pallas_call(finish_kernel, grid=(4,), out_shape=jax.ShapeDtypeStruct((...  12.1 us

profile of v3, /device:TPU:1, one launch (start us, length us, event | category | flops | bytes accessed | tf_op | source)
XLA Modules:
  0.0 62.7 jit_solution(9644221239749289533)
XLA Ops:
  0.0 50.6 %spread.1 = (bf16[2,32,2,64,128]{4,3,2,1,0:T(8,128)(2,1)}, s32[2,32,1,128]{3,2,1,0:T(1,128)}) custom-call(s32[2,1,128]{2,1,0:T(1,128)} %bitcast.11, s32[1,32]{1,0:T(1,128)} %counts_ref.1, bf16[64,512]{1,0:T(8,128)(2,1)} %bitcast.9, bf16[64,512]{1,0:T(8,128)(2,1)} %bitcast.10, s32[2,1,128]{2,1,0:T(1,128)} %bitcast.12), custom_call_target="tpu_custom_call" | custom-call | tf_op jit(solution)/shard_map/spread/pallas_call | solution.py:288
  50.6 12.1 %finish.1 = f32[2,4,512,128]{3,2,1,0:T(8,128)} custom-call(s32[2,32,1,128]{3,2,1,0:T(1,128)} %get-tuple-element.7.offs_ref, bf16[2,32,2,64,128]{4,3,2,1,0:T(8,128)(2,1)} %get-tuple-element.8.lists_ref, f32[2,128,128]{2,1,0:T(8,128)} %constant.4.clone.twist_ref, bf16[256,256]{1,0:T(8,128)(2,1)} %constant.5.clone.matrix_ref), custom_call_target="tpu_custom_call" | custom-call | tf_op jit(solution)/shard_map/finish/pallas_call | solution.py:434

commit v4 on v3

--- a/solution.py
+++ b/solution.py
@@ -15,6 +15,8 @@
 NBLK = 64
 LANES = 128
 TILES = G // LANES
+SLABS = 2
+UNROLL = 8
 MESH = pl.DeviceIdType.MESH
 F32 = jnp.float32
 BF16 = jnp.bfloat16
@@ -240,6 +242,14 @@
     send(0, 1, 15)
     own = pltpu.make_async_copy(send_ref.at[0, 0, 15], recv_ref.at[0, band], own_sem.at[0])
     own.start()
+
+    def tell(j, carry):
+        offsets(0, target(j)).start()
+        offsets(1, target(j)).start()
+        return carry
+
+    lax.fori_loop(1, S, tell, 0)
+    offsets(1, band).start()
     for copy in inputs():
         copy.wait()
     numbers = pltpu.make_async_copy(table_ref.at[1], number_ref.at[1], number_sem.at[1])
@@ -252,13 +262,6 @@
     twins = pltpu.make_async_copy(send_ref.at[1, 0, 15], recv_ref.at[0, twin], own_sem.at[2])
     twins.start()
 
-    def tell(j, carry):
-        offsets(0, target(j)).start()
-        offsets(1, target(j)).start()
-        return carry
-
-    lax.fori_loop(1, S, tell, 0)
-    offsets(1, band).start()
     own_offs.wait()
     own.wait()
     twins.wait()
@@ -341,13 +344,17 @@
     return [add(e, o) for e, o in zip(even, odd)] + [sub(e, o) for e, o in zip(even, odd)]
 
 
-def finish_kernel(offs_ref, lists_ref, twist_ref, matrix_ref, out_ref, mid_ref, sec_ref, *slabs):
+def finish_kernel(offs_ref, lists_any, twist_ref, matrix_ref, out_ref, mid_ref, sec_ref, lists_ref, sem, *slabs):
     part = pl.program_id(0)
 
     @pl.when(part == 0)
     def _():
         band = lax.axis_index("band")
-        zero = jnp.zeros((8, LANES), F32)
+        fetches = [
+            pltpu.make_async_copy(lists_any.at[half], lists_ref.at[half], sem.at[half]) for half in range(2)
+        ]
+        for fetch in fetches:
+            fetch.start()
 
         def clear(t, carry):
             for slab in slabs:
@@ -357,12 +364,14 @@
         lax.fori_loop(0, TILES + 1, clear, 0)
         lane = lax.broadcasted_iota(jnp.int32, (8, LANES), 1)
         for half in range(2):
+            fetches[half].wait()
             base = ((31 - band if half else band) & 15) * CAP
 
             def place(i, carry, half=half, base=base):
                 for group in range(2):
                     values = lists_ref[half, i, group].astype(F32)
-                    for j, slab in enumerate(slabs):
+                    for j in range(4):
+                        slab = slabs[j % len(slabs)]
                         start = offs_ref[half, i, 0, base + (group * 4 + j)]
                         if half:
                             start = G - S - start
@@ -372,15 +381,19 @@
                         inner = (lane >= first) & (lane < first + S)
                         outer = lane < first + (S - LANES)
                         for p in range(0, 2 * S, 8):
-                            slab[tile, p : p + 8] += jnp.where(inner, turned[p : p + 8], zero)
-                            slab[tile + 1, p : p + 8] += jnp.where(outer, turned[p : p + 8], zero)
+                            for at, mask in ((tile, inner), (tile + 1, outer)):
+                                here = slab.at[at, p : p + 8]
+                                pltpu.store(here, here[...] + turned[p : p + 8], mask=mask)
                 return carry
 
-            lax.fori_loop(0, S, place, 0, unroll=2)
+            lax.fori_loop(0, S, place, 0, unroll=UNROLL)
 
     def folded(t, row):
         at = pl.ds(pl.multiple_of(row, 8), 8)
-        return (slabs[0][t, at] + slabs[1][t, at]) + (slabs[2][t, at] + slabs[3][t, at])
+        total = slabs[0][t, at]
+        for slab in slabs[1:]:
+            total = total + slab[t, at]
+        return total
 
     for t2 in range(8):
         made = fft8([(folded(8 * t1 + t2, 8 * part), folded(8 * t1 + t2, 8 * part + S)) for t1 in range(8)])
@@ -435,13 +448,20 @@
         finish_kernel,
         grid=(4,),
         out_shape=jax.ShapeDtypeStruct((2, 4, 8 * TILES, LANES), F32),
-        in_specs=[pl.BlockSpec(memory_space=pltpu.SMEM), vmem, vmem, vmem],
+        in_specs=[
+            pl.BlockSpec(memory_space=pltpu.SMEM),
+            pl.BlockSpec(memory_space=pl.ANY),
+            vmem,
+            vmem,
+        ],
         out_specs=pl.BlockSpec((2, 1, 8 * TILES, LANES), lambda i: (0, i, 0, 0)),
         scratch_shapes=[
             pltpu.VMEM((2, TILES, 8, LANES), F32),
             pltpu.VMEM((2, 8 * TILES, LANES), F32),
+            pltpu.VMEM((2, S, 2, 2 * S, LANES), BF16),
+            pltpu.SemaphoreType.DMA((2,)),
         ]
-        + [pltpu.VMEM((TILES + 1, 2 * S, LANES), F32)] * 4,
+        + [pltpu.VMEM((TILES + 1, 2 * S, LANES), F32)] * SLABS,
         name="finish",
     )(offsets, lists, *map(jnp.asarray, tables()))
 

time: 62.9 us -> 58.1 us (0.924)
  Pallas kernels: 62.7 us -> 57.9 us
    pallas_call x1, Pallas kernels: 12.1 us -> 9.65 us  [finish(): pl.pallas_call(finish_kernel, grid=(4,), out_shape=jax.ShapeDtypeStruct((...]
    pallas_call x1, Pallas kernels: 50.6 us -> 48.3 us  [spread_lists(): pl.pallas_call(spread, out_shape=(jax.ShapeDtypeStruct((2, S, 2, 2 * S, L...]
where the time goes in v4:
time: 58.1 us; the launch traced here: 57.9 us
  Pallas kernels  57.9 us (100%)
    pallas_call x1, Pallas kernels, spread_lists(): pl.pallas_call(spread, out_shape=(jax.ShapeDtypeStruct((2, S, 2, 2 * S, L...  48.3 us
    pallas_call x1, Pallas kernels, finish(): pl.pallas_call(finish_kernel, grid=(4,), out_shape=jax.ShapeDtypeStruct((...  9.65 us

profile of v4, /device:TPU:1, one launch (start us, length us, event | category | flops | bytes accessed | tf_op | source)
XLA Modules:
  0.0 57.9 jit_solution(15982460406838794605)
XLA Ops:
  0.0 48.3 %spread.1 = (bf16[2,32,2,64,128]{4,3,2,1,0:T(8,128)(2,1)}, s32[2,32,1,128]{3,2,1,0:T(1,128)}) custom-call(s32[2,1,128]{2,1,0:T(1,128)} %bitcast.11, s32[1,32]{1,0:T(1,128)} %counts_ref.1, bf16[64,512]{1,0:T(8,128)(2,1)} %bitcast.9, bf16[64,512]{1,0:T(8,128)(2,1)} %bitcast.10, s32[2,1,128]{2,1,0:T(1,128)} %bitcast.12), custom_call_target="tpu_custom_call" | custom-call | tf_op jit(solution)/shard_map/spread/pallas_call | solution.py:291
  48.3 9.7 %finish.1 = f32[2,4,512,128]{3,2,1,0:T(8,128)} custom-call(s32[2,32,1,128]{3,2,1,0:T(1,128)} %get-tuple-element.7.offs_ref, bf16[2,32,2,64,128]{4,3,2,1,0:T(8,128)(2,1)} %get-tuple-element.8.lists_any, f32[2,128,128]{2,1,0:T(8,128)} %constant.4.clone.twist_ref, bf16[256,256]{1,0:T(8,128)(2,1)} %constant.5.clone.matrix_ref), custom_call_target="tpu_custom_call" | custom-call | tf_op jit(solution)/shard_map/finish/pallas_call | solution.py:447

commit v5 on v4

--- a/solution.py
+++ b/solution.py
@@ -15,6 +15,8 @@
 NBLK = 64
 LANES = 128
 TILES = G // LANES
+OWN = 20
+TURN = 8
 SLABS = 2
 UNROLL = 8
 MESH = pl.DeviceIdType.MESH
@@ -156,19 +158,20 @@
 
     def blocks(begin, end):
         def some_blocks(i, carry):
-            for j in range(4):
-                one_block(i * 4 + j)
+            for j in range(TURN):
+                one_block(i * TURN + j)
             return carry
 
-        lax.fori_loop(begin // 4, end // 4, some_blocks, 0)
-
-    def served(half, q):
-        dz = 2 - half - (q // 4 + 3 - half) % 4
+        lax.fori_loop(begin // TURN, end // TURN, some_blocks, 0)
+
+    def served(which, half, q):
+        k = q // 4 + 2 * which
+        dz = (2 - k // 2) * (2 * (k % 2) - 1)
         return ((z + dz + 8) % 8) * 4 + (x + 3 - q % 4) % 4
 
     def expand(which, q):
         for half in range(2):
-            e = served(half, q)
+            e = served(which, half, q)
             d = e + half * (31 - 2 * e)
             live = number_ref[which, 2, 0, d]
             for group in range(2):
@@ -181,15 +184,15 @@
                 value = sub_ref[half, idx[3]]
                 for i in range(3):
                     value = jnp.where(lane == i, sub_ref[half, idx[i]], value)
-                send_ref[which, half, q, group] = value
+                send_ref[half, OWN * which + q, group] = value
 
     def send(which, half, q):
         pltpu.make_async_remote_copy(
-            src_ref=send_ref.at[which, half, q],
+            src_ref=send_ref.at[half, OWN * which + q],
             dst_ref=recv_ref.at[half, twin if which else band],
             send_sem=send_sem.at[half],
             recv_sem=recv_sem.at[half],
-            device_id=device(half, served(half, q)),
+            device_id=device(half, served(which, half, q)),
             device_id_type=MESH,
         ).start()
 
@@ -202,7 +205,7 @@
             send(which, 1, q - 1)
             return carry
 
-        lax.fori_loop(1, 16, pass_on, 0)
+        lax.fori_loop(1, S - OWN if which else OWN, pass_on, 0)
 
     def inputs():
         pairs = ((vis_ref, data_ref.at[0]), (coord_ref, data_ref.at[1]), (table_ref.at[0], table_ref.at[1]))
@@ -239,8 +242,8 @@
     own_offs = pltpu.make_async_copy(offs_ref.at[band // 16], roff_ref.at[0, band], own_sem.at[1])
     own_offs.start()
     send_lists(0)
-    send(0, 1, 15)
-    own = pltpu.make_async_copy(send_ref.at[0, 0, 15], recv_ref.at[0, band], own_sem.at[0])
+    send(0, 1, OWN - 1)
+    own = pltpu.make_async_copy(send_ref.at[0, OWN - 1], recv_ref.at[0, band], own_sem.at[0])
     own.start()
 
     def tell(j, carry):
@@ -258,8 +261,8 @@
     blocks(0, NBLK)
     numbers.wait()
     send_lists(1)
-    send(1, 1, 15)
-    twins = pltpu.make_async_copy(send_ref.at[1, 0, 15], recv_ref.at[0, twin], own_sem.at[2])
+    send(1, 1, S - OWN - 1)
+    twins = pltpu.make_async_copy(send_ref.at[0, S - 1], recv_ref.at[0, twin], own_sem.at[2])
     twins.start()
 
     own_offs.wait()
@@ -300,7 +303,7 @@
             pltpu.VMEM((NBLK, 2 * K), F32),
             pltpu.VMEM((2, 5, 2, NBLK, K), F32),
             pltpu.VMEM((2, NBLK + 1, 2 * S, LANES), BF16),
-            pltpu.VMEM((2, 2, 16, 2, 2 * S, LANES), BF16),
+            pltpu.VMEM((2, S, 2, 2 * S, LANES), BF16),
             pltpu.VMEM((2, NBLK, 2 * K), BF16),
             pltpu.VMEM((2, 3, 1, LANES), jnp.int32),
             pltpu.SMEM((2, 3, 1, LANES), jnp.int32),

time: 58.1 us -> 57.5 us (0.990)
  Pallas kernels: 57.9 us -> 57.3 us
    pallas_call x1, Pallas kernels: 48.3 us -> 47.6 us  [spread_lists(): pl.pallas_call(spread, out_shape=(jax.ShapeDtypeStruct((2, S, 2, 2 * S, L...]
where the time goes in v5:
time: 57.5 us; the launch traced here: 57.3 us
  Pallas kernels  57.3 us (100%)
    pallas_call x1, Pallas kernels, spread_lists(): pl.pallas_call(spread, out_shape=(jax.ShapeDtypeStruct((2, S, 2, 2 * S, L...  47.6 us
    pallas_call x1, Pallas kernels, finish(): pl.pallas_call(finish_kernel, grid=(4,), out_shape=jax.ShapeDtypeStruct((...  9.66 us

profile of v5, /device:TPU:1, one launch (start us, length us, event | category | flops | bytes accessed | tf_op | source)
XLA Modules:
  0.0 57.3 jit_solution(1428682259976296293)
XLA Ops:
  0.0 47.6 %spread.1 = (bf16[2,32,2,64,128]{4,3,2,1,0:T(8,128)(2,1)}, s32[2,32,1,128]{3,2,1,0:T(1,128)}) custom-call(s32[2,1,128]{2,1,0:T(1,128)} %bitcast.11, s32[1,32]{1,0:T(1,128)} %counts_ref.1, bf16[64,512]{1,0:T(8,128)(2,1)} %bitcast.9, bf16[64,512]{1,0:T(8,128)(2,1)} %bitcast.10, s32[2,1,128]{2,1,0:T(1,128)} %bitcast.12), custom_call_target="tpu_custom_call" | custom-call | tf_op jit(solution)/shard_map/spread/pallas_call | solution.py:294
  47.6 9.7 %finish.1 = f32[2,4,512,128]{3,2,1,0:T(8,128)} custom-call(s32[2,32,1,128]{3,2,1,0:T(1,128)} %get-tuple-element.7.offs_ref, bf16[2,32,2,64,128]{4,3,2,1,0:T(8,128)(2,1)} %get-tuple-element.8.lists_any, f32[2,128,128]{2,1,0:T(8,128)} %constant.4.clone.twist_ref, bf16[256,256]{1,0:T(8,128)(2,1)} %constant.5.clone.matrix_ref), custom_call_target="tpu_custom_call" | custom-call | tf_op jit(solution)/shard_map/finish/pallas_call | solution.py:450

commit v6 on v5

--- a/solution.py
+++ b/solution.py
@@ -347,88 +347,101 @@
     return [add(e, o) for e, o in zip(even, odd)] + [sub(e, o) for e, o in zip(even, odd)]
 
 
-def finish_kernel(offs_ref, lists_any, twist_ref, matrix_ref, out_ref, mid_ref, sec_ref, lists_ref, sem, *slabs):
-    part = pl.program_id(0)
-
-    @pl.when(part == 0)
-    def _():
-        band = lax.axis_index("band")
-        fetches = [
-            pltpu.make_async_copy(lists_any.at[half], lists_ref.at[half], sem.at[half]) for half in range(2)
-        ]
-        for fetch in fetches:
-            fetch.start()
-
-        def clear(t, carry):
-            for slab in slabs:
-                slab[t] = jnp.zeros((2 * S, LANES), F32)
+def finish_kernel(offs_ref, lists_any, twist_ref, matrix_ref, out_any, out_ref, mid_ref, sec_ref, lists_ref, sem, *slabs):
+    band = lax.axis_index("band")
+    fetches = [
+        pltpu.make_async_copy(lists_any.at[half], lists_ref.at[half], sem.at[half]) for half in range(2)
+    ]
+    for fetch in fetches:
+        fetch.start()
+
+    def clear(t, carry):
+        for slab in slabs:
+            slab[t] = jnp.zeros((2 * S, LANES), F32)
+        return carry
+
+    lax.fori_loop(0, TILES + 1, clear, 0)
+    lane = lax.broadcasted_iota(jnp.int32, (8, LANES), 1)
+    for half in range(2):
+        fetches[half].wait()
+        base = ((31 - band if half else band) & 15) * CAP
+
+        def place(i, carry, half=half, base=base):
+            for group in range(2):
+                values = lists_ref[half, i, group].astype(F32)
+                for j in range(4):
+                    slab = slabs[j % len(slabs)]
+                    start = offs_ref[half, i, 0, base + (group * 4 + j)]
+                    if half:
+                        start = G - S - start
+                    tile = lax.shift_right_logical(start, 7)
+                    first = start & (LANES - 1)
+                    turned = pltpu.roll(values, (first - S * j) & (LANES - 1), 1)
+                    inner = (lane >= first) & (lane < first + S)
+                    outer = lane < first + (S - LANES)
+                    for p in range(0, 2 * S, 8):
+                        for at, mask in ((tile, inner), (tile + 1, outer)):
+                            here = slab.at[at, p : p + 8]
+                            pltpu.store(here, here[...] + turned[p : p + 8], mask=mask)
             return carry
 
-        lax.fori_loop(0, TILES + 1, clear, 0)
-        lane = lax.broadcasted_iota(jnp.int32, (8, LANES), 1)
-        for half in range(2):
-            fetches[half].wait()
-            base = ((31 - band if half else band) & 15) * CAP
-
-            def place(i, carry, half=half, base=base):
-                for group in range(2):
-                    values = lists_ref[half, i, group].astype(F32)
-                    for j in range(4):
-                        slab = slabs[j % len(slabs)]
-                        start = offs_ref[half, i, 0, base + (group * 4 + j)]
-                        if half:
-                            start = G - S - start
-                        tile = lax.shift_right_logical(start, 7)
-                        first = start & (LANES - 1)
-                        turned = pltpu.roll(values, (first - S * j) & (LANES - 1), 1)
-                        inner = (lane >= first) & (lane < first + S)
-                        outer = lane < first + (S - LANES)
-                        for p in range(0, 2 * S, 8):
-                            for at, mask in ((tile, inner), (tile + 1, outer)):
-                                here = slab.at[at, p : p + 8]
-                                pltpu.store(here, here[...] + turned[p : p + 8], mask=mask)
-                return carry
-
-            lax.fori_loop(0, S, place, 0, unroll=UNROLL)
+        lax.fori_loop(0, S, place, 0, unroll=UNROLL)
 
     def folded(t, row):
-        at = pl.ds(pl.multiple_of(row, 8), 8)
-        total = slabs[0][t, at]
+        total = slabs[0][t, row : row + 8]
         for slab in slabs[1:]:
-            total = total + slab[t, at]
+            total = total + slab[t, row : row + 8]
         return total
 
-    for t2 in range(8):
-        made = fft8([(folded(8 * t1 + t2, 8 * part), folded(8 * t1 + t2, 8 * part + S)) for t1 in range(8)])
+    def tiles(part):
+        for t2 in range(8):
+            made = fft8([(folded(8 * t1 + t2, 8 * part), folded(8 * t1 + t2, 8 * part + S)) for t1 in range(8)])
+            for q1 in range(8):
+                re, im = made[q1]
+                angle = -2 * math.pi * t2 * q1 / 64
+                if t2 * q1:
+                    c, s = math.cos(angle), math.sin(angle)
+                    re, im = re * c - im * s, im * c + re * s
+                mid_ref[part, 0, q1 * 8 + t2] = re
+                mid_ref[part, 1, q1 * 8 + t2] = im
         for q1 in range(8):
-            re, im = made[q1]
-            angle = -2 * math.pi * t2 * q1 / 64
-            if t2 * q1:
-                c, s = math.cos(angle), math.sin(angle)
-                re, im = re * c - im * s, im * c + re * s
-            mid_ref[0, q1 * 8 + t2] = re
-            mid_ref[1, q1 * 8 + t2] = im
-    for q1 in range(8):
-        made = fft8([(mid_ref[0, q1 * 8 + t2], mid_ref[1, q1 * 8 + t2]) for t2 in range(8)])
-        for q2 in range(8):
-            at = (q1 + 8 * q2) * 8
-            sec_ref[0, at : at + 8] = made[q2][0]
-            sec_ref[1, at : at + 8] = made[q2][1]
+            made = fft8([(mid_ref[part, 0, q1 * 8 + t2], mid_ref[part, 1, q1 * 8 + t2]) for t2 in range(8)])
+            for q2 in range(8):
+                at = (q1 + 8 * q2) * 8
+                sec_ref[part, 0, at : at + 8] = made[q2][0]
+                sec_ref[part, 1, at : at + 8] = made[q2][1]
+
     matrix = matrix_ref[...]
-    for r in range(8):
-        sr = sec_ref[0, pl.ds(r, TILES, stride=8), :]
-        si = sec_ref[1, pl.ds(r, TILES, stride=8), :]
-        zr, zi = [], []
-        for k in range(2):
-            tr = twist_ref[0, k * TILES : (k + 1) * TILES]
-            ti = twist_ref[1, k * TILES : (k + 1) * TILES]
-            zr.append(sr * tr - si * ti)
-            zi.append(si * tr + sr * ti)
-        full = jnp.concatenate([jnp.concatenate(zr, 0), jnp.concatenate(zi, 0)], 1).astype(BF16)
-        made = lax.dot_general(matrix, full, (((1,), (1,)), ((), ())), preferred_element_type=F32)
-        made = made[:LANES] + made[LANES:]
-        out_ref[0, 0, pl.ds(r, TILES, stride=8), :] = made[:TILES]
-        out_ref[1, 0, pl.ds(r, TILES, stride=8), :] = made[TILES:]
+
+    def rows(part):
+        for r in range(8):
+            at = pl.ds(r, TILES, stride=8)
+            sr = sec_ref[part, 0, at, :]
+            si = sec_ref[part, 1, at, :]
+            zr, zi = [], []
+            for k in range(2):
+                tr = twist_ref[0, k * TILES : (k + 1) * TILES]
+                ti = twist_ref[1, k * TILES : (k + 1) * TILES]
+                zr.append(sr * tr - si * ti)
+                zi.append(si * tr + sr * ti)
+            full = jnp.concatenate([jnp.concatenate(zr, 0), jnp.concatenate(zi, 0)], 1).astype(BF16)
+            made = lax.dot_general(matrix, full, (((1,), (1,)), ((), ())), preferred_element_type=F32)
+            made = made[:LANES] + made[LANES:]
+            out_ref[0, part, at, :] = made[:TILES]
+            out_ref[1, part, at, :] = made[TILES:]
+
+    leaves = []
+    for part in range(4):
+        tiles(part)
+        if part:
+            rows(part - 1)
+            leaves.append(pltpu.make_async_copy(out_ref.at[:, part - 1], out_any.at[:, part - 1], sem.at[1 + part]))
+            leaves[-1].start()
+    rows(3)
+    leaves.append(pltpu.make_async_copy(out_ref.at[:, 3], out_any.at[:, 3], sem.at[5]))
+    leaves[-1].start()
+    for leave in leaves:
+        leave.wait()
 
 
 def tables():
@@ -449,7 +462,6 @@
     vmem = pl.BlockSpec(memory_space=pltpu.VMEM)
     return pl.pallas_call(
         finish_kernel,
-        grid=(4,),
         out_shape=jax.ShapeDtypeStruct((2, 4, 8 * TILES, LANES), F32),
         in_specs=[
             pl.BlockSpec(memory_space=pltpu.SMEM),
@@ -457,12 +469,13 @@
             vmem,
             vmem,
         ],
-        out_specs=pl.BlockSpec((2, 1, 8 * TILES, LANES), lambda i: (0, i, 0, 0)),
+        out_specs=pl.BlockSpec(memory_space=pl.ANY),
         scratch_shapes=[
-            pltpu.VMEM((2, TILES, 8, LANES), F32),
-            pltpu.VMEM((2, 8 * TILES, LANES), F32),
+            pltpu.VMEM((2, 4, 8 * TILES, LANES), F32),
+            pltpu.VMEM((4, 2, TILES, 8, LANES), F32),
+            pltpu.VMEM((4, 2, 8 * TILES, LANES), F32),
             pltpu.VMEM((2, S, 2, 2 * S, LANES), BF16),
-            pltpu.SemaphoreType.DMA((2,)),
+            pltpu.SemaphoreType.DMA((6,)),
         ]
         + [pltpu.VMEM((TILES + 1, 2 * S, LANES), F32)] * SLABS,
         name="finish",

time: 57.5 us -> 56.7 us (0.986)
  Pallas kernels: 57.3 us -> 56.5 us
    pallas_call x1, Pallas kernels: 9.66 us -> 8.9 us  [finish(): pl.pallas_call(finish_kernel, out_shape=jax.ShapeDtypeStruct((2, 4, 8 * T...]
where the time goes in v6:
time: 56.7 us; the launch traced here: 56.6 us
  Pallas kernels  56.5 us (100%)
    pallas_call x1, Pallas kernels, spread_lists(): pl.pallas_call(spread, out_shape=(jax.ShapeDtypeStruct((2, S, 2, 2 * S, L...  47.6 us
    pallas_call x1, Pallas kernels, finish(): pl.pallas_call(finish_kernel, out_shape=jax.ShapeDtypeStruct((2, 4, 8 * T...  8.9 us

profile of v6, /device:TPU:1, one launch (start us, length us, event | category | flops | bytes accessed | tf_op | source)
XLA Modules:
  0.0 56.6 jit_solution(5417366572620816608)
XLA Ops:
  0.0 47.6 %spread.1 = (bf16[2,32,2,64,128]{4,3,2,1,0:T(8,128)(2,1)}, s32[2,32,1,128]{3,2,1,0:T(1,128)}) custom-call(s32[2,1,128]{2,1,0:T(1,128)} %bitcast.11, s32[1,32]{1,0:T(1,128)} %counts_ref.1, bf16[64,512]{1,0:T(8,128)(2,1)} %bitcast.9, bf16[64,512]{1,0:T(8,128)(2,1)} %bitcast.10, s32[2,1,128]{2,1,0:T(1,128)} %bitcast.12), custom_call_target="tpu_custom_call" | custom-call | tf_op jit(solution)/shard_map/spread/pallas_call | solution.py:294
  47.6 8.9 %finish.1 = f32[2,4,512,128]{3,2,1,0:T(8,128)} custom-call(s32[2,32,1,128]{3,2,1,0:T(1,128)} %get-tuple-element.7.offs_ref, bf16[2,32,2,64,128]{4,3,2,1,0:T(8,128)(2,1)} %get-tuple-element.8.lists_any, f32[2,128,128]{2,1,0:T(8,128)} %constant.4.clone.twist_ref, bf16[256,256]{1,0:T(8,128)(2,1)} %constant.5.clone.matrix_ref), custom_call_target="tpu_custom_call" | custom-call | tf_op jit(solution)/shard_map/finish/pallas_call | solution.py:463

commit v7 on v6

--- a/solution.py
+++ b/solution.py
@@ -61,7 +61,9 @@
     twin = ((z + 4) % 8) * 4 + x
 
     def target(j):
-        return ((z + j // 4) % 8) * 4 + (x + j % 4) % 4
+        k = j // 4
+        dz = 4 + ((k + 1) // 2) * (2 * (k % 2) - 1)
+        return ((z + dz) % 8) * 4 + (x + 3 - j % 4) % 4
 
     def device(half, e):
         return (e, plane + half * (7 - 2 * plane))
@@ -73,7 +75,7 @@
         pl.semaphore_signal(barrier, inc=1, device_id=device(1, target(j)), device_id_type=MESH)
         return carry
 
-    lax.fori_loop(1, S, greet, 0)
+    lax.fori_loop(0, S - 1, greet, 0)
     pl.semaphore_signal(barrier, inc=1, device_id=device(1, band), device_id_type=MESH)
 
     table_ref[0, 0:2] = index_ref[...]
@@ -251,7 +253,7 @@
         offsets(1, target(j)).start()
         return carry
 
-    lax.fori_loop(1, S, tell, 0)
+    lax.fori_loop(0, S - 1, tell, 0)
     offsets(1, band).start()
     for copy in inputs():
         copy.wait()
@@ -360,7 +362,7 @@
             slab[t] = jnp.zeros((2 * S, LANES), F32)
         return carry
 
-    lax.fori_loop(0, TILES + 1, clear, 0)
+    lax.fori_loop(0, TILES + 1, clear, 0, unroll=5)
     lane = lax.broadcasted_iota(jnp.int32, (8, LANES), 1)
     for half in range(2):
         fetches[half].wait()

time: 56.7 us -> 57.8 us (1.019)
  Pallas kernels: 56.5 us -> 57.6 us
    pallas_call x1, Pallas kernels: 47.6 us -> 48.7 us  [spread_lists(): pl.pallas_call(spread, out_shape=(jax.ShapeDtypeStruct((2, S, 2, 2 * S, L...]
where the time goes in v7:
time: 57.8 us; the launch traced here: 57.6 us
  Pallas kernels  57.6 us (100%)
    pallas_call x1, Pallas kernels, spread_lists(): pl.pallas_call(spread, out_shape=(jax.ShapeDtypeStruct((2, S, 2, 2 * S, L...  48.7 us
    pallas_call x1, Pallas kernels, finish(): pl.pallas_call(finish_kernel, out_shape=jax.ShapeDtypeStruct((2, 4, 8 * T...  8.91 us

profile of v7, /device:TPU:1, one launch (start us, length us, event | category | flops | bytes accessed | tf_op | source)
XLA Modules:
  0.0 57.6 jit_solution(2793087437905392438)
XLA Ops:
  0.0 48.7 %spread.1 = (bf16[2,32,2,64,128]{4,3,2,1,0:T(8,128)(2,1)}, s32[2,32,1,128]{3,2,1,0:T(1,128)}) custom-call(s32[2,1,128]{2,1,0:T(1,128)} %bitcast.11, s32[1,32]{1,0:T(1,128)} %counts_ref.1, bf16[64,512]{1,0:T(8,128)(2,1)} %bitcast.9, bf16[64,512]{1,0:T(8,128)(2,1)} %bitcast.10, s32[2,1,128]{2,1,0:T(1,128)} %bitcast.12), custom_call_target="tpu_custom_call" | custom-call | tf_op jit(solution)/shard_map/spread/pallas_call | solution.py:296
  48.7 8.9 %finish.1 = f32[2,4,512,128]{3,2,1,0:T(8,128)} custom-call(s32[2,32,1,128]{3,2,1,0:T(1,128)} %get-tuple-element.7.offs_ref, bf16[2,32,2,64,128]{4,3,2,1,0:T(8,128)(2,1)} %get-tuple-element.8.lists_any, f32[2,128,128]{2,1,0:T(8,128)} %constant.4.clone.twist_ref, bf16[256,256]{1,0:T(8,128)(2,1)} %constant.5.clone.matrix_ref), custom_call_target="tpu_custom_call" | custom-call | tf_op jit(solution)/shard_map/finish/pallas_call | solution.py:465
